TPU v7x, 128 devices: a whole 4x4x4 slice. The times are simulated.
128 devices in a mesh: rows: 16 (over x, z_lo, core), cols: 8 (over z_hi, y).
Axes of the slice: x: 4, y: 4, z: 4 (z_hi: 2, z_lo: 2; z = z_hi * 2 + z_lo), core: 2. Of those that a mesh axis runs over, the one named last changes fastest.
Arguments:
- krylov: bfloat16 [32768, 256], P(('rows', 'cols')), may hold values from -6 to 6
- geometry: float32 [7, 32768], P(None, ('rows', 'cols')), may hold values from -1 to 2, as said below
- corr_index: int32 [8, 32768], P(None, ('rows', 'cols')), may hold values from 0 to 32767, as said below
- corr_weight: float32 [16, 32768], P(None, ('rows', 'cols')), may hold values from -1.5 to 1.5
- blades: int32 [128], replicated, may hold values from 3 to 8
- harmonic: int32 [128], replicated, may hold values from 1 to 4
- observer_angles: float32 [2, 8192], replicated, may hold values from -3.140625 to 3.140625
Outputs:
- residual: float32 [32768, 256], P(('rows', 'cols'))
- far_field: float32 [8192, 256], P(('rows', 'cols'))
Inputs may be any that keep to these rules, and one draw needn't show every extreme that they name: `geometry`: centers lie on a duct of radius about 1 with heights 0 to 2 and on a centerbody of radius 0.35; normals have unit length; areas are positive. corr_index[c, i] lies in the same aligned block of 256 consecutive panels as panel i.
All inputs are finite; a program needn't handle non-finite values.
Results may differ from a plain program's by a relative error of at most 0.0029.
Values may be sent and summed in bfloat16 or wider, within the bound.
A program may use at most 64 MiB of HBM per device.

v0:
```python
import math

import jax
import jax.numpy as jnp
from jax import lax
from jax.sharding import PartitionSpec as P

NS = 64


wavenumber = 20.0
cycle_radius = 0.7
cycle_height = 1.0
four_pi = 4.0 * math.pi


def in_order(tiles, dim):
    tiles = jnp.moveaxis(tiles, 0, dim)
    shape = tiles.shape
    return tiles.reshape(*shape[:dim], shape[dim] * shape[dim + 1], *shape[dim + 2 :])


def from_everyone(x, axis):
    devices = lax.axis_size(axis)
    return lax.all_to_all(jnp.broadcast_to(x[None], (devices, *x.shape)), axis, 0, 0, tiled=True)


def collect(x, axis, dim):
    return in_order(from_everyone(x, axis), dim)


def cut_along(x, dim, devices):
    shape = x.shape
    tiles = x.reshape(*shape[:dim], devices, shape[dim] // devices, *shape[dim + 1 :])
    return jnp.moveaxis(tiles, dim, 0)


def sent_and_summed(x, axis, dim):
    devices = lax.axis_size(axis)
    tiles = lax.all_to_all(cut_along(x, dim, devices), axis, 0, 0, tiled=True)
    return jnp.sum(tiles, axis=0)


def green_parts(r_sq):
    inverse = lax.rsqrt(r_sq)
    phase = wavenumber * r_sq * inverse
    g_re = jnp.cos(phase) * inverse / four_pi
    g_im = jnp.sin(phase) * inverse / four_pi
    f_re = (-g_re * inverse - wavenumber * g_im) * inverse
    f_im = (-g_im * inverse + wavenumber * g_re) * inverse
    return (g_re, g_im, f_re, f_im)


def panel_tile(row_geom, col_geom, row_ids, col_ids, soft_sq):
    dx = row_geom[0][:, None] - col_geom[0][None, :]
    dy = row_geom[1][:, None] - col_geom[1][None, :]
    dz = row_geom[2][:, None] - col_geom[2][None, :]
    r_sq = dx * dx + dy * dy + dz * dz + soft_sq
    g_re, g_im, f_re, f_im = green_parts(r_sq)
    along_col = -(dx * col_geom[3][None, :] + dy * col_geom[4][None, :] + dz * col_geom[5][None, :])
    along_row = (
        dx * row_geom[3][:, None] + dy * row_geom[4][:, None] + dz * row_geom[5][:, None]
    ) / wavenumber
    area = col_geom[6][None, :]
    t_re = area * (f_re * along_col - f_im * along_row)
    t_im = area * (f_re * along_row + f_im * along_col)
    same = row_ids[:, None] == col_ids[None, :]
    zeros = jnp.zeros_like(t_re)
    return (
        jnp.where(same, zeros, t_re).astype(jnp.bfloat16),
        jnp.where(same, zeros, t_im).astype(jnp.bfloat16),
    )


def apply_tile(t_re, t_im, vectors):
    nvec = vectors.shape[1] // 2
    first = jnp.dot(t_re, vectors, preferred_element_type=jnp.float32)
    second = jnp.dot(t_im, vectors, preferred_element_type=jnp.float32)
    return jnp.concatenate(
        [first[:, :nvec] - second[:, nvec:], first[:, nvec:] + second[:, :nvec]], axis=1
    )


def far_tile(angles, geom):
    sin_t = jnp.sin(angles[0])
    dir_x = sin_t * jnp.cos(angles[1])
    dir_y = sin_t * jnp.sin(angles[1])
    dir_z = jnp.cos(angles[0])
    along = (
        dir_x[:, None] * geom[0][None, :]
        + dir_y[:, None] * geom[1][None, :]
        + dir_z[:, None] * geom[2][None, :]
    )
    normal_part = (
        dir_x[:, None] * geom[3][None, :]
        + dir_y[:, None] * geom[4][None, :]
        + dir_z[:, None] * geom[5][None, :]
    )
    phase = -wavenumber * along
    scale = geom[6][None, :] * wavenumber * normal_part
    t_re = scale * jnp.sin(phase)
    t_im = -scale * jnp.cos(phase)
    return (t_re.astype(jnp.bfloat16), t_im.astype(jnp.bfloat16))


def incident(geom, blades, harmonic):
    angle = 2.0 * math.pi * jnp.arange(NS, dtype=jnp.float32) / NS
    src_x = cycle_radius * jnp.cos(angle)
    src_y = cycle_radius * jnp.sin(angle)
    dx = geom[0][:, None] - src_x[None, :]
    dy = geom[1][:, None] - src_y[None, :]
    dz = geom[2][:, None] - cycle_height
    r_sq = dx * dx + dy * dy + dz * dz
    g_re, g_im, f_re, f_im = green_parts(r_sq)
    normal_part = (
        dx * geom[3][:, None] + dy * geom[4][:, None] + dz * geom[5][:, None]
    ) / wavenumber
    h_re = g_re - f_im * normal_part
    h_im = g_im + f_re * normal_part
    modes = (blades * harmonic).astype(jnp.float32)
    e_re = jnp.cos(angle[:, None] * modes[None, :])
    e_im = jnp.sin(angle[:, None] * modes[None, :])
    high = lax.Precision.HIGHEST
    b_re = jnp.dot(h_re, e_re, precision=high) - jnp.dot(h_im, e_im, precision=high)
    b_im = jnp.dot(h_re, e_im, precision=high) + jnp.dot(h_im, e_re, precision=high)
    return jnp.concatenate([b_re, b_im], axis=1)


def correction(values, index_local, weights):
    count = index_local.shape[0]
    nvec = values.shape[1] // 2
    nearby = values[index_local]
    w_re = weights[:count][:, :, None]
    w_im = weights[count:][:, :, None]
    part_re = jnp.sum(w_re * nearby[:, :, :nvec] - w_im * nearby[:, :, nvec:], axis=0)
    part_im = jnp.sum(w_re * nearby[:, :, nvec:] + w_im * nearby[:, :, :nvec], axis=0)
    return jnp.concatenate([part_re, part_im], axis=1)


def local(krylov, geometry, corr_index, corr_weight, blades, harmonic, observer_angles):
    nrows = lax.axis_size("rows")
    ncols = lax.axis_size("cols")
    row_at = lax.axis_index("rows")
    col_at = lax.axis_index("cols")
    piece = krylov.shape[0]
    width = krylov.shape[1]
    panels = piece * nrows * ncols
    soft_sq = 4.0 / panels
    row_geom = collect(geometry, "cols", 1)
    col_geom = collect(geometry, "rows", 1)
    col_vectors = collect(krylov, "rows", 0)
    row_ids = row_at * (ncols * piece) + jnp.arange(ncols * piece, dtype=jnp.int32)
    col_pos = jnp.arange(nrows * piece, dtype=jnp.int32)
    col_ids = (col_pos // piece * ncols + col_at) * piece + col_pos % piece
    block = math.gcd(piece * lax.axis_size("cols"), 256)

    def one_block(step):
        begin = step * block
        geom = lax.dynamic_slice_in_dim(row_geom, begin, block, 1)
        ids = lax.dynamic_slice_in_dim(row_ids, begin, block, 0)
        t_re, t_im = panel_tile(geom, col_geom, ids, col_ids, soft_sq)
        return apply_tile(t_re, t_im, col_vectors)

    applied = sent_and_summed(
        lax.map(
            one_block, jnp.arange(piece * lax.axis_size("cols") // block, dtype=jnp.int32)
        ).reshape(piece * lax.axis_size("cols"), width),
        "cols",
        0,
    )
    first_panel = (row_at * ncols + col_at) * piece
    values = krylov.astype(jnp.float32)
    near = correction(values, corr_index - first_panel, corr_weight)
    source = incident(geometry, blades, harmonic)
    residual = source - (0.5 * values + near + applied)
    obs_each = observer_angles.shape[1] // (nrows * ncols)
    group_first = row_at * (ncols * obs_each)
    group_block = math.gcd(obs_each * lax.axis_size("cols"), 512)

    def one_group(step):
        angles = lax.dynamic_slice_in_dim(
            observer_angles, group_first + step * group_block, group_block, 1
        )
        t_re, t_im = far_tile(angles, col_geom)
        return apply_tile(t_re, t_im, col_vectors)

    far_field = sent_and_summed(
        lax.map(
            one_group, jnp.arange(obs_each * lax.axis_size("cols") // group_block, dtype=jnp.int32)
        ).reshape(obs_each * lax.axis_size("cols"), width),
        "cols",
        0,
    )
    return (residual, far_field)


def solution(mesh):
    placed = (
        P(("rows", "cols"), None),
        P(None, ("rows", "cols")),
        P(None, ("rows", "cols")),
        P(None, ("rows", "cols")),
        P(),
        P(),
        P(),
    )
    return jax.shard_map(
        local,
        mesh=mesh,
        in_specs=placed,
        out_specs=(P(("rows", "cols"), None), P(("rows", "cols"), None)),
        check_vma=False,
    )
```

profile of v0, /device:TPU:1, one launch (start us, length us, event | category | flops | bytes accessed | tf_op | source)
XLA Modules:
  0.0 525.8 jit_solution(17245875917401464316)
XLA Ops:
  0.6 1.4 broadcast_in_dim.27
  2.0 7.2 %all-to-all-start = ((f32[16,7,256]{2,1,0:T(8,128)}), f32[16,7,256]{2,1,0:T(8,128)S(1)}, u32[]{:S(2)}, u32[]{:S(2)}) async-start(f32[16,7,256]{2,1,0:T(8,128)} %broadcast_in_dim.27), calls=%async_computation | async-start | bytes 262144 | tf_op jit(solution)/shard_map/all_to_all | solution.py:25
  9.9 0.7 fusion.109
  10.6 0.9 cosine_multiply_fusion.1
  11.5 3.8 all-to-all-done
  15.3 2.4 broadcast_in_dim.29
  17.7 4.0 all-to-all-start.2
  21.8 32.7 %multiply_convert_fusion.10 = bf16[512,4096]{1,0:T(8,128)(2,1)} fusion(f32[4096]{0:T(1024)S(1)} %bitcast.128, f32[4096]{0:T(1024)S(1)} %bitcast.118, f32[4096]{0:T(1024)S(1)} %bitcast.120, f32[4096]{0:T(1024)S(1)} %bitcast.122, f32[512]{0:T(512)S(1)} %bitcast.146, f32[4096]{0:T(1024)S(1)} %bitcast.124, f32[512]{0:T(512)S(1)} %bitcast.148, ...), kind=kLoop, calls=%fused_computation.72.clone.clone.1 | loop fusion | flops 31457280 | bytes 4315136 | tf_op jit(solution)/shard_map/while/body/eval_jaxpr/dot_general | solution.py:78
  54.5 32.9 %multiply_convert_fusion.9 = bf16[512,4096]{1,0:T(8,128)(2,1)} fusion(f32[4096]{0:T(1024)S(1)} %bitcast.129, f32[4096]{0:T(1024)S(1)} %bitcast.119, f32[4096]{0:T(1024)S(1)} %bitcast.121, f32[4096]{0:T(1024)S(1)} %bitcast.123, f32[512]{0:T(512)S(1)} %bitcast.147, f32[4096]{0:T(1024)S(1)} %bitcast.125, f32[512]{0:T(512)S(1)} %bitcast.149, ...), kind=kLoop, calls=%fused_computation.73.clone.clone.1 | loop fusion | flops 29360128 | bytes 4315136 | tf_op jit(solution)/shard_map/while/body/eval_jaxpr/dot_general | solution.py:77
  88.0 7.2 %all-to-all-start.1 = ((f32[8,7,256]{2,1,0:T(8,128)}), f32[8,7,256]{2,1,0:T(8,128)S(1)}, u32[]{:S(2)}, u32[]{:S(2)}) async-start(f32[8,7,256]{2,1,0:T(8,128)} %broadcast_in_dim.28), calls=%async_computation.1 | async-start | bytes 131072 | tf_op jit(solution)/shard_map/all_to_all | solution.py:25
  95.2 3.6 fusion.52
  98.9 1.3 fusion.51
  100.3 1.0 copy.26
  101.9 6.0 %all-to-all-start.4 = ((f32[8,64,256]{2,1,0:T(8,128)}), f32[8,64,256]{2,1,0:T(8,128)S(1)}, u32[]{:S(2)}, u32[]{:S(2)}) async-start(f32[8,64,256]{2,1,0:T(8,128)} %bitcast.22), calls=%async_computation.4 | async-start | bytes 1048576 | tf_op jit(solution)/shard_map/all_to_all | solution.py:40
  108.0 379.4 %while.18 = (s32[]{:T(128)}, f32[8,256,256]{1,2,0:T(8,128)}, s32[8]{0:T(128)S(1)}, s32[2048]{0:T(1024)S(1)}, f32[7,4096]{1,0:T(8,128)S(1)}, /*index=5*/f32[7,204...) while((s32[]{:T(128)}, f32[8,256,256]{1,2,0:T(8,128)}, ...), condition=%wide.region_3.4_spmd.clone, body=%wide.region_2.3_spmd.clone.sunk | while | flops 1166213120 | bytes 14954815 | solution.py:165
  125.6 20.6 %fusion.146 = bf16[256,4096]{1,0:T(8,128)(2,1)S(1)} fusion(f32[256]{0:T(256)S(1)} %bitcast.142, f32[256]{0:T(256)S(1)} %bitcast.134, f32[256]{0:T(256)S(1)} %bitcast.136, f32[4096]{0:T(1024)S(1)} %bitcast.104, f32[4096]{0:T(1024)S(1)} %bitcast.106, f32[4096]{0:T(1024)S(1)} %bitcast.108, f32[4096]{0:T(1024)S(1)} %bitcast.110, ...), kind=kLoop, calls=%fused_computation.14.clone.clone.1.clone.1 | loop fusion | flops 46137344 | bytes 2235392 | tf_op jit(solution)/shard_map/while/body/eval_jaxpr/dot_general | solution.py:78
  146.1 1.0 fusion.147
  147.1 20.6 %fusion.148 = bf16[256,4096]{1,0:T(8,128)(2,1)S(1)} fusion(f32[256]{0:T(256)S(1)} %bitcast.143, f32[256]{0:T(256)S(1)} %bitcast.135, f32[256]{0:T(256)S(1)} %bitcast.137, f32[4096]{0:T(1024)S(1)} %bitcast.105, f32[4096]{0:T(1024)S(1)} %bitcast.107, f32[4096]{0:T(1024)S(1)} %bitcast.109, f32[4096]{0:T(1024)S(1)} %bitcast.111, ...), kind=kLoop, calls=%fused_computation.13.clone.clone.1.clone.1 | loop fusion | flops 46137344 | bytes 2235392 | tf_op jit(solution)/shard_map/while/body/eval_jaxpr/dot_general | solution.py:77
  167.7 1.0 fusion.149
  168.7 0.7 fusion.150
  171.0 20.6 %fusion.146 = bf16[256,4096]{1,0:T(8,128)(2,1)S(1)} fusion(f32[256]{0:T(256)S(1)} %bitcast.142, f32[256]{0:T(256)S(1)} %bitcast.134, f32[256]{0:T(256)S(1)} %bitcast.136, f32[4096]{0:T(1024)S(1)} %bitcast.104, f32[4096]{0:T(1024)S(1)} %bitcast.106, f32[4096]{0:T(1024)S(1)} %bitcast.108, f32[4096]{0:T(1024)S(1)} %bitcast.110, ...), kind=kLoop, calls=%fused_computation.14.clone.clone.1.clone.1 | loop fusion | flops 46137344 | bytes 2235392 | tf_op jit(solution)/shard_map/while/body/eval_jaxpr/dot_general | solution.py:78
  191.5 1.0 fusion.147
  192.5 20.6 %fusion.148 = bf16[256,4096]{1,0:T(8,128)(2,1)S(1)} fusion(f32[256]{0:T(256)S(1)} %bitcast.143, f32[256]{0:T(256)S(1)} %bitcast.135, f32[256]{0:T(256)S(1)} %bitcast.137, f32[4096]{0:T(1024)S(1)} %bitcast.105, f32[4096]{0:T(1024)S(1)} %bitcast.107, f32[4096]{0:T(1024)S(1)} %bitcast.109, f32[4096]{0:T(1024)S(1)} %bitcast.111, ...), kind=kLoop, calls=%fused_computation.13.clone.clone.1.clone.1 | loop fusion | flops 46137344 | bytes 2235392 | tf_op jit(solution)/shard_map/while/body/eval_jaxpr/dot_general | solution.py:77
  213.1 1.0 fusion.149
  214.1 0.7 fusion.150
  216.4 20.6 %fusion.146 = bf16[256,4096]{1,0:T(8,128)(2,1)S(1)} fusion(f32[256]{0:T(256)S(1)} %bitcast.142, f32[256]{0:T(256)S(1)} %bitcast.134, f32[256]{0:T(256)S(1)} %bitcast.136, f32[4096]{0:T(1024)S(1)} %bitcast.104, f32[4096]{0:T(1024)S(1)} %bitcast.106, f32[4096]{0:T(1024)S(1)} %bitcast.108, f32[4096]{0:T(1024)S(1)} %bitcast.110, ...), kind=kLoop, calls=%fused_computation.14.clone.clone.1.clone.1 | loop fusion | flops 46137344 | bytes 2235392 | tf_op jit(solution)/shard_map/while/body/eval_jaxpr/dot_general | solution.py:78
  236.9 1.0 fusion.147
  237.9 20.6 %fusion.148 = bf16[256,4096]{1,0:T(8,128)(2,1)S(1)} fusion(f32[256]{0:T(256)S(1)} %bitcast.143, f32[256]{0:T(256)S(1)} %bitcast.135, f32[256]{0:T(256)S(1)} %bitcast.137, f32[4096]{0:T(1024)S(1)} %bitcast.105, f32[4096]{0:T(1024)S(1)} %bitcast.107, f32[4096]{0:T(1024)S(1)} %bitcast.109, f32[4096]{0:T(1024)S(1)} %bitcast.111, ...), kind=kLoop, calls=%fused_computation.13.clone.clone.1.clone.1 | loop fusion | flops 46137344 | bytes 2235392 | tf_op jit(solution)/shard_map/while/body/eval_jaxpr/dot_general | solution.py:77
  258.5 1.0 fusion.149
  259.5 0.8 fusion.150
  261.8 20.6 %fusion.146 = bf16[256,4096]{1,0:T(8,128)(2,1)S(1)} fusion(f32[256]{0:T(256)S(1)} %bitcast.142, f32[256]{0:T(256)S(1)} %bitcast.134, f32[256]{0:T(256)S(1)} %bitcast.136, f32[4096]{0:T(1024)S(1)} %bitcast.104, f32[4096]{0:T(1024)S(1)} %bitcast.106, f32[4096]{0:T(1024)S(1)} %bitcast.108, f32[4096]{0:T(1024)S(1)} %bitcast.110, ...), kind=kLoop, calls=%fused_computation.14.clone.clone.1.clone.1 | loop fusion | flops 46137344 | bytes 2235392 | tf_op jit(solution)/shard_map/while/body/eval_jaxpr/dot_general | solution.py:78
  282.4 1.0 fusion.147
  283.3 20.6 %fusion.148 = bf16[256,4096]{1,0:T(8,128)(2,1)S(1)} fusion(f32[256]{0:T(256)S(1)} %bitcast.143, f32[256]{0:T(256)S(1)} %bitcast.135, f32[256]{0:T(256)S(1)} %bitcast.137, f32[4096]{0:T(1024)S(1)} %bitcast.105, f32[4096]{0:T(1024)S(1)} %bitcast.107, f32[4096]{0:T(1024)S(1)} %bitcast.109, f32[4096]{0:T(1024)S(1)} %bitcast.111, ...), kind=kLoop, calls=%fused_computation.13.clone.clone.1.clone.1 | loop fusion | flops 46137344 | bytes 2235392 | tf_op jit(solution)/shard_map/while/body/eval_jaxpr/dot_general | solution.py:77
  303.9 1.0 fusion.149
  304.9 0.7 fusion.150
  307.2 20.6 %fusion.146 = bf16[256,4096]{1,0:T(8,128)(2,1)S(1)} fusion(f32[256]{0:T(256)S(1)} %bitcast.142, f32[256]{0:T(256)S(1)} %bitcast.134, f32[256]{0:T(256)S(1)} %bitcast.136, f32[4096]{0:T(1024)S(1)} %bitcast.104, f32[4096]{0:T(1024)S(1)} %bitcast.106, f32[4096]{0:T(1024)S(1)} %bitcast.108, f32[4096]{0:T(1024)S(1)} %bitcast.110, ...), kind=kLoop, calls=%fused_computation.14.clone.clone.1.clone.1 | loop fusion | flops 46137344 | bytes 2235392 | tf_op jit(solution)/shard_map/while/body/eval_jaxpr/dot_general | solution.py:78
  327.8 1.0 fusion.147
  328.7 20.6 %fusion.148 = bf16[256,4096]{1,0:T(8,128)(2,1)S(1)} fusion(f32[256]{0:T(256)S(1)} %bitcast.143, f32[256]{0:T(256)S(1)} %bitcast.135, f32[256]{0:T(256)S(1)} %bitcast.137, f32[4096]{0:T(1024)S(1)} %bitcast.105, f32[4096]{0:T(1024)S(1)} %bitcast.107, f32[4096]{0:T(1024)S(1)} %bitcast.109, f32[4096]{0:T(1024)S(1)} %bitcast.111, ...), kind=kLoop, calls=%fused_computation.13.clone.clone.1.clone.1 | loop fusion | flops 46137344 | bytes 2235392 | tf_op jit(solution)/shard_map/while/body/eval_jaxpr/dot_general | solution.py:77
  349.3 1.0 fusion.149
  350.3 0.7 fusion.150
  352.6 20.6 %fusion.146 = bf16[256,4096]{1,0:T(8,128)(2,1)S(1)} fusion(f32[256]{0:T(256)S(1)} %bitcast.142, f32[256]{0:T(256)S(1)} %bitcast.134, f32[256]{0:T(256)S(1)} %bitcast.136, f32[4096]{0:T(1024)S(1)} %bitcast.104, f32[4096]{0:T(1024)S(1)} %bitcast.106, f32[4096]{0:T(1024)S(1)} %bitcast.108, f32[4096]{0:T(1024)S(1)} %bitcast.110, ...), kind=kLoop, calls=%fused_computation.14.clone.clone.1.clone.1 | loop fusion | flops 46137344 | bytes 2235392 | tf_op jit(solution)/shard_map/while/body/eval_jaxpr/dot_general | solution.py:78
  373.1 1.0 fusion.147
  374.1 20.6 %fusion.148 = bf16[256,4096]{1,0:T(8,128)(2,1)S(1)} fusion(f32[256]{0:T(256)S(1)} %bitcast.143, f32[256]{0:T(256)S(1)} %bitcast.135, f32[256]{0:T(256)S(1)} %bitcast.137, f32[4096]{0:T(1024)S(1)} %bitcast.105, f32[4096]{0:T(1024)S(1)} %bitcast.107, f32[4096]{0:T(1024)S(1)} %bitcast.109, f32[4096]{0:T(1024)S(1)} %bitcast.111, ...), kind=kLoop, calls=%fused_computation.13.clone.clone.1.clone.1 | loop fusion | flops 46137344 | bytes 2235392 | tf_op jit(solution)/shard_map/while/body/eval_jaxpr/dot_general | solution.py:77
  394.7 1.0 fusion.149
  395.7 0.7 fusion.150
  398.0 20.6 %fusion.146 = bf16[256,4096]{1,0:T(8,128)(2,1)S(1)} fusion(f32[256]{0:T(256)S(1)} %bitcast.142, f32[256]{0:T(256)S(1)} %bitcast.134, f32[256]{0:T(256)S(1)} %bitcast.136, f32[4096]{0:T(1024)S(1)} %bitcast.104, f32[4096]{0:T(1024)S(1)} %bitcast.106, f32[4096]{0:T(1024)S(1)} %bitcast.108, f32[4096]{0:T(1024)S(1)} %bitcast.110, ...), kind=kLoop, calls=%fused_computation.14.clone.clone.1.clone.1 | loop fusion | flops 46137344 | bytes 2235392 | tf_op jit(solution)/shard_map/while/body/eval_jaxpr/dot_general | solution.py:78
  418.5 1.0 fusion.147
  419.5 20.6 %fusion.148 = bf16[256,4096]{1,0:T(8,128)(2,1)S(1)} fusion(f32[256]{0:T(256)S(1)} %bitcast.143, f32[256]{0:T(256)S(1)} %bitcast.135, f32[256]{0:T(256)S(1)} %bitcast.137, f32[4096]{0:T(1024)S(1)} %bitcast.105, f32[4096]{0:T(1024)S(1)} %bitcast.107, f32[4096]{0:T(1024)S(1)} %bitcast.109, f32[4096]{0:T(1024)S(1)} %bitcast.111, ...), kind=kLoop, calls=%fused_computation.13.clone.clone.1.clone.1 | loop fusion | flops 46137344 | bytes 2235392 | tf_op jit(solution)/shard_map/while/body/eval_jaxpr/dot_general | solution.py:77
  440.1 1.0 fusion.149
  441.1 0.7 fusion.150
  443.4 20.6 %fusion.146 = bf16[256,4096]{1,0:T(8,128)(2,1)S(1)} fusion(f32[256]{0:T(256)S(1)} %bitcast.142, f32[256]{0:T(256)S(1)} %bitcast.134, f32[256]{0:T(256)S(1)} %bitcast.136, f32[4096]{0:T(1024)S(1)} %bitcast.104, f32[4096]{0:T(1024)S(1)} %bitcast.106, f32[4096]{0:T(1024)S(1)} %bitcast.108, f32[4096]{0:T(1024)S(1)} %bitcast.110, ...), kind=kLoop, calls=%fused_computation.14.clone.clone.1.clone.1 | loop fusion | flops 46137344 | bytes 2235392 | tf_op jit(solution)/shard_map/while/body/eval_jaxpr/dot_general | solution.py:78
  463.9 1.0 fusion.147
  464.9 20.6 %fusion.148 = bf16[256,4096]{1,0:T(8,128)(2,1)S(1)} fusion(f32[256]{0:T(256)S(1)} %bitcast.143, f32[256]{0:T(256)S(1)} %bitcast.135, f32[256]{0:T(256)S(1)} %bitcast.137, f32[4096]{0:T(1024)S(1)} %bitcast.105, f32[4096]{0:T(1024)S(1)} %bitcast.107, f32[4096]{0:T(1024)S(1)} %bitcast.109, f32[4096]{0:T(1024)S(1)} %bitcast.111, ...), kind=kLoop, calls=%fused_computation.13.clone.clone.1.clone.1 | loop fusion | flops 46137344 | bytes 2235392 | tf_op jit(solution)/shard_map/while/body/eval_jaxpr/dot_general | solution.py:77
  485.5 1.0 fusion.149
  486.5 0.7 fusion.150
  487.5 6.5 %all-to-all-start.3 = ((f32[8,256,256]{1,2,0:T(8,128)}), f32[8,256,256]{1,2,0:T(8,128)}, u32[]{:S(2)}, u32[]{:S(2)}) async-start(f32[8,256,256]{1,2,0:T(8,128)} %get-tuple-element.143), calls=%async_computation.3 | async-start | bytes 4194304 | tf_op jit(solution)/shard_map/all_to_all | solution.py:40
  494.3 6.6 %gather_fusion = f32[2048,256]{1,0:T(8,128)S(1)} fusion(f32[256,256]{1,0:T(8,128)S(1)} %copy.23, s32[2048]{0:T(1024)S(1)} %broadcast_clamp_fusion), kind=kCustom, calls=%fused_computation | custom fusion | bytes 4202496 | tf_op jit(solution)/shard_map/gather | solution.py:132
  500.9 0.7 subtract_reduce_fusion
  502.7 0.7 fusion.74
  503.4 0.7 convolution_add_fusion
  504.1 0.7 convolution_subtract_fusion
  505.5 17.2 %all-to-all-done.3 = f32[8,256,256]{1,2,0:T(8,128)} async-done(((f32[8,256,256]{1,2,0:T(8,128)}), f32[8,256,256]{1,2,0:T(8,128)}, u32[]{:S(2)}, u32[]{:S(2)}) %all-to-all-start.3) | async-done | bytes 2097184 | tf_op jit(solution)/shard_map/all_to_all | solution.py:40
  522.7 1.8 reduce_sum.38
  524.5 0.8 copy.27
  (82 shorter events, 11.1 us)
Async XLA Ops:
  2.0 13.3 %all-to-all-start = ((f32[16,7,256]{2,1,0:T(8,128)}), f32[16,7,256]{2,1,0:T(8,128)S(1)}, u32[]{:S(2)}, u32[]{:S(2)}) async-start(f32[16,7,256]{2,1,0:T(8,128)} %broadcast_in_dim.27), calls=%async_computation | async-start | bytes 262144 | tf_op jit(solution)/shard_map/all_to_all | solution.py:25
  17.7 69.7 %all-to-all-start.2 = ((bf16[16,256,256]{2,1,0:T(8,128)(2,1)}), bf16[16,256,256]{2,1,0:T(8,128)(2,1)S(1)}, u32[]{:S(2)}, u32[]{:S(2)}) async-start(bf16[16,256,256]{2,1,0:T(8,128)(2,1)} %broadcast_in_dim.29), calls=%async_computation.2 | async-start | bytes 4194304 | tf_op jit(solution)/shard_map/all_to_all | solution.py:25
  21.8 65.6 %copy-start.2 = (f32[7,256]{1,0:T(8,128)S(1)}, f32[7,256]{1,0:T(8,128)}, u32[]{:S(2)}) copy-start(f32[7,256]{1,0:T(8,128)} %param.10) | copy-start | bytes 21508
  88.0 13.9 %all-to-all-start.1 = ((f32[8,7,256]{2,1,0:T(8,128)}), f32[8,7,256]{2,1,0:T(8,128)S(1)}, u32[]{:S(2)}, u32[]{:S(2)}) async-start(f32[8,7,256]{2,1,0:T(8,128)} %broadcast_in_dim.28), calls=%async_computation.1 | async-start | bytes 131072 | tf_op jit(solution)/shard_map/all_to_all | solution.py:25
  95.2 3.6 copy-start
  101.9 385.5 %all-to-all-start.4 = ((f32[8,64,256]{2,1,0:T(8,128)}), f32[8,64,256]{2,1,0:T(8,128)S(1)}, u32[]{:S(2)}, u32[]{:S(2)}) async-start(f32[8,64,256]{2,1,0:T(8,128)} %bitcast.22), calls=%async_computation.4 | async-start | bytes 1048576 | tf_op jit(solution)/shard_map/all_to_all | solution.py:40
  487.5 6.6 %copy-start.1 = (bf16[256,256]{1,0:T(8,128)(2,1)S(1)}, bf16[256,256]{1,0:T(8,128)(2,1)}, u32[]{:S(2)}) copy-start(bf16[256,256]{1,0:T(8,128)(2,1)} %param.9) | copy-start | bytes 393220
  487.5 35.2 %all-to-all-start.3 = ((f32[8,256,256]{1,2,0:T(8,128)}), f32[8,256,256]{1,2,0:T(8,128)}, u32[]{:S(2)}, u32[]{:S(2)}) async-start(f32[8,256,256]{1,2,0:T(8,128)} %get-tuple-element.143), calls=%async_computation.3 | async-start | bytes 4194304 | tf_op jit(solution)/shard_map/all_to_all | solution.py:40
  494.2 7.7 %copy-start.3 = (s32[128]{0:T(128)S(1)}, s32[128]{0:T(128)}, u32[]{:S(2)}) copy-start(s32[128]{0:T(128)} %param.13) | copy-start | bytes 1540
  494.2 7.7 %copy-start.4 = (s32[128]{0:T(128)S(1)}, s32[128]{0:T(128)}, u32[]{:S(2)}) copy-start(s32[128]{0:T(128)} %param.14) | copy-start | bytes 1540
where the time goes:
time: 533 us; the launch traced here: 526 us
  other arithmetic  406 us (76%)
  starting transfers between devices  30.9 us (6%)
  matrix products  23.4 us (4%)
  loops' own time  21.9 us (4%)
  waiting for transfers between devices  21.6 us (4%)
  local copies, waits for them, and re-layouts  20.7 us (4%)
    dot_general x9, other arithmetic, apply_tile(): first = jnp.dot(t_re, vectors, preferred_element_type=jnp.float32)  197 us
    dot_general x9, other arithmetic, apply_tile(): second = jnp.dot(t_im, vectors, preferred_element_type=jnp.float32)  197 us
    another operation x1, loops' own time, local(): lax.map(one_block, jnp.arange(piece * lax.axis_size('cols') // block, dty...  21.9 us
    all_to_all x3, starting transfers between devices, from_everyone(): lax.all_to_all(jnp.broadcast_to(x[None], (devices, *x.shape)), axis, 0, 0...  18.3 us
    all_to_all x2, waiting for transfers between devices, sent_and_summed(): tiles = lax.all_to_all(cut_along(x, dim, devices), axis, 0, 0, tiled=True)  17.2 us
    all_to_all x2, starting transfers between devices, sent_and_summed(): tiles = lax.all_to_all(cut_along(x, dim, devices), axis, 0, 0, tiled=True)  12.6 us
    dot_general x9, matrix products, apply_tile(): second = jnp.dot(t_im, vectors, preferred_element_type=jnp.float32)  11.4 us
  transfers between devices with their start and end apart: 5, of which 3 were waited for; matrix products, arithmetic and copies ran while one was open for 84% of the time, Pallas kernels for 0%

commit v1 on v0

v1 whole, which is shorter than its diff:
```python
import functools
import math

import jax
import jax.numpy as jnp
from jax import lax
from jax.experimental import pallas as pl
from jax.experimental.pallas import tpu as pltpu
from jax.sharding import PartitionSpec as P

BF = jnp.bfloat16
F32 = jnp.float32
NS = 64
LANES = 128

wavenumber = 20.0
cycle_radius = 0.7
cycle_height = 1.0
four_pi = 4.0 * math.pi
two_pi = 2.0 * math.pi
kappa = wavenumber / two_pi

dot = functools.partial(jnp.dot, preferred_element_type=F32)


def pieces(x):
    first = x.astype(BF).astype(F32)
    rest = x - first
    second = rest.astype(BF).astype(F32)
    return first, second, (rest - second).astype(BF).astype(F32)


def left_stack(x):
    a, b, c = pieces(x)
    return jnp.concatenate([a, a, b, a, c, b], axis=0)


def right_stack(x):
    a, b, c = pieces(x)
    return jnp.concatenate([a, b, a, c, a, b], axis=0).astype(BF)


def panel_rows(g):
    row = lax.broadcasted_iota(jnp.int32, g.shape, 0)
    center = row < 3
    normal = pltpu.roll(g, 5, 0)
    c_sq = jnp.sum(jnp.where(center, g * g, 0.0), axis=0, keepdims=True)
    n_c = jnp.sum(jnp.where(center, g * normal, 0.0), axis=0, keepdims=True)
    return row, center, normal, c_sq, n_c, g[6:7]


def left_features(g, soft_sq):
    row, center, normal, c_sq, n_c, _ = panel_rows(g)
    size = (kappa * kappa) * (c_sq + soft_sq)
    one = jnp.where(row == 3, 1.0, jnp.where(row == 4, size, 0.0))
    two = jnp.where(row == 3, n_c, 0.0)
    return (
        left_stack(jnp.where(center, g, one)),
        left_stack(jnp.where(center, normal, two)),
    )


def right_features(g):
    row, center, normal, c_sq, n_c, area = panel_rows(g)
    scale = area * (kappa * kappa / four_pi)
    k_sq = kappa * kappa
    r_sq = jnp.where(
        center, -2.0 * k_sq * g, jnp.where(row == 3, k_sq * c_sq, jnp.where(row == 4, 1.0, 0.0))
    )
    along_col = jnp.where(
        center, -wavenumber * scale * normal, jnp.where(row == 3, wavenumber * scale * n_c, 0.0)
    )
    along_row = jnp.where(center, scale * g, jnp.where(row == 3, -scale, 0.0))
    far_turns = jnp.where(center, kappa * g, 0.0)
    far_scale = jnp.where(center, -wavenumber * area * normal, 0.0)
    return [right_stack(v) for v in (r_sq, along_col, along_row, far_turns, far_scale)]


def operator_tile(r_sq, along_col, along_row):
    inv = lax.rsqrt(r_sq)
    turns = r_sq * inv
    part = (turns - jnp.round(turns)).astype(BF)
    u = inv.astype(BF)
    a = along_col.astype(BF)
    b = along_row.astype(BF)

    def const(v):
        return jnp.asarray(v, BF)

    z = part * part
    sin_poly = (z * const(SIN[2]) + const(SIN[1])) * z + const(SIN[0])
    cos_poly = (z * const(COS[2]) + const(COS[1])) * z + const(COS[0])
    s = (part * u) * sin_poly
    c = u * cos_poly
    re = u * u - s * s
    im = s * c
    w = u * const(1.0 / two_pi)
    p = b - w * a
    q = a + w * b
    return re * p - im * q, re * q + im * p


root2 = math.sqrt(2.0)
SIN = [root2 * v for v in (3.14064003, -5.1369052, 2.29954689)]
COS = [root2 * v for v in (0.99940322, -4.89118661, 3.5838431)]


def far_values(turns, scale):
    part = turns - jnp.round(turns)
    z = part * part
    s = part * (((z * -0.55463616 + 2.54189901) * z + -5.16714279) * z + 3.14158202)
    c = ((z * -1.22212692 + 4.04128377) * z + -4.93393801) * z + 0.9999933
    s2 = s + s
    return (scale * (s2 * c)).astype(BF), (scale * (1.0 - s2 * s)).astype(BF)


def sin_cos(turns):
    part = turns - jnp.round(turns)
    quarter = jnp.round(4.0 * part)
    y = (part - 0.25 * quarter) * two_pi
    z = y * y
    s = y * (1.0 + z * (-1.0 / 6 + z * (1.0 / 120 + z * (-1.0 / 5040 + z * (1.0 / 362880)))))
    c = 1.0 + z * (-0.5 + z * (1.0 / 24 + z * (-1.0 / 720 + z * (1.0 / 40320))))
    odd = jnp.abs(quarter) == 1.0
    sin_v = jnp.where(odd, c, s)
    cos_v = jnp.where(odd, s, c)
    sin_v = jnp.where((quarter == -1.0) | (jnp.abs(quarter) == 2.0), -sin_v, sin_v)
    cos_v = jnp.where((quarter == 1.0) | (jnp.abs(quarter) == 2.0), -cos_v, cos_v)
    return sin_v, cos_v


ROWS = 512
COLS = 512
SUB = 16


def compute(row_geom, col_geom, vectors, angles, own, out, far_out, left_a, left_b, rights, x2, planes, tiles, acc):
    n_rows = row_geom.shape[1]
    n_cols = col_geom.shape[1]
    steps = n_cols // COLS
    half = COLS // LANES
    soft_sq = 4.0 / own[2]

    la, lb = left_features(row_geom[...], soft_sq)
    left_a[pl.ds(0, n_rows), :] = la.T.astype(BF)
    left_b[...] = lb.T.astype(BF)
    t, p = angles[0:1, :] * (1.0 / two_pi), angles[1:2, :] * (1.0 / two_pi)
    sin_t, cos_t = sin_cos(t)
    sin_p, cos_p = sin_cos(p)
    e = jnp.concatenate([sin_t * cos_p, sin_t * sin_p, cos_t, jnp.zeros((5, t.shape[1]), F32)], axis=0)
    left_a[pl.ds(n_rows, t.shape[1]), :] = left_stack(e).T.astype(BF)
    for ref, v in zip(rights, right_features(col_geom[...])):
        ref[...] = v
    for i in range(steps):
        x = vectors[pl.ds(i * COLS, COLS), :]
        x2[pl.ds(i * 2 * COLS, COLS), :] = x
        x2[pl.ds(i * 2 * COLS + COLS, COLS), :] = jnp.concatenate([-x[:, LANES:], x[:, :LANES]], axis=1)

    def geometry(first, step, far, into):
        cols = pl.ds(pl.multiple_of(step * COLS, COLS), COLS)
        la = left_a[pl.ds(pl.multiple_of(first, ROWS), ROWS), :]
        if far:
            into[0][...] = dot(la, rights[3][:, cols])
            into[1][...] = dot(la, rights[4][:, cols])
        else:
            lb = left_b[pl.ds(pl.multiple_of(first, ROWS), ROWS), :]
            into[0][...] = dot(la, rights[0][:, cols])
            into[1][...] = dot(la, rights[1][:, cols])
            into[2][...] = dot(lb, rights[2][:, cols])

    def values(step, far, frm, tile):
        for r in range(0, ROWS, SUB):
            rows = pl.ds(r, SUB)
            if far:
                re, im = far_values(frm[0][rows, :], frm[1][rows, :])
            else:
                re, im = operator_tile(frm[0][rows, :], frm[1][rows, :], frm[2][rows, :])
            for h in range(half):
                tile[step * 2 * half + h, rows, :] = re[:, h * LANES:(h + 1) * LANES]
                tile[step * 2 * half + half + h, rows, :] = im[:, h * LANES:(h + 1) * LANES]

    def product(step, tile):
        lhs = jnp.concatenate([tile[step * 2 * half + h] for h in range(2 * half)], axis=1)
        xs = pl.ds(pl.multiple_of(step * 2 * COLS, 2 * COLS), 2 * COLS)
        acc[...] += dot(lhs, x2[xs, :])

    blocks = n_rows // ROWS
    seq = [(n_rows, True)] + [(b * ROWS, False) for b in range(blocks)]
    for ph in range(len(seq) + 1):
        gen = ph < len(seq)
        mul = ph > 0
        if gen:
            first, far = seq[ph]
            geometry(first, 0, far, planes[0])
        if mul:
            acc[...] = jnp.zeros_like(acc)

        @pl.loop(0, steps // 2)
        def _(h):
            for par in range(2):
                step = 2 * h + par
                if gen:
                    geometry(first, lax.rem(step + 1, steps), far, planes[1 - par])
                    values(step, far, planes[par], tiles[ph % 2])
                if mul:
                    product(step, tiles[(ph - 1) % 2])

        if gen and not far:
            @pl.when(own[0] // ROWS == first // ROWS)
            def _():
                rows = pl.ds(pl.multiple_of(own[0] % ROWS, 256), 256)
                same = lax.broadcasted_iota(jnp.int32, (256, LANES), 0)
                lane = lax.broadcasted_iota(jnp.int32, (256, LANES), 1)
                for h in range(2):
                    for part in range(2):
                        at = own[1] // COLS * 2 * half + part * half + own[1] % COLS // LANES + h
                        v = tiles[ph % 2][at, rows, :].astype(F32)
                        tiles[ph % 2][at, rows, :] = jnp.where(same == lane + h * LANES, 0.0, v).astype(BF)
        if mul:
            first, far = seq[ph - 1]
            if far:
                far_out[...] = acc[...]
            else:
                out[pl.ds(first, ROWS), :] = acc[...]


def tile_products(row_geom, col_geom, vectors, angles, row_first, col_first, panels):
    n_rows, n_cols, n_obs = row_geom.shape[1], col_geom.shape[1], angles.shape[1]
    pad = lambda g: jnp.concatenate([g, jnp.zeros((1, g.shape[1]), F32)], axis=0)

    def body(own_ref, rg, cg, x, an, out, far_out, la, lb, r0, r1, r2, r3, r4, x2, p0, p1, p2, p3, p4, p5, t0, t1, acc):
        compute(rg, cg, x, an, (own_ref[0], own_ref[1], panels), out, far_out, la, lb, (r0, r1, r2, r3, r4), x2,
                ((p0, p1, p2), (p3, p4, p5)), (t0, t1), acc)

    vm = pl.BlockSpec(memory_space=pltpu.VMEM)
    return pl.pallas_call(
        body,
        out_shape=(jax.ShapeDtypeStruct((n_rows, 256), F32), jax.ShapeDtypeStruct((n_obs, 256), F32)),
        in_specs=[pl.BlockSpec(memory_space=pltpu.SMEM), vm, vm, vm, vm],
        out_specs=(vm, vm),
        scratch_shapes=[pltpu.VMEM((n_rows + n_obs, 48), BF), pltpu.VMEM((n_rows, 48), BF)]
        + [pltpu.VMEM((48, n_cols), BF)] * 5
        + [pltpu.VMEM((2 * n_cols, 256), BF)]
        + [pltpu.VMEM((ROWS, COLS), F32)] * 6
        + [pltpu.VMEM((2 * n_cols // LANES, ROWS, LANES), BF)] * 2
        + [pltpu.VMEM((ROWS, 256), F32)],
        compiler_params=pltpu.CompilerParams(vmem_limit_bytes=60 << 20),
        name="tile_products",
    )(jnp.stack([row_first, col_first]).astype(jnp.int32), pad(row_geom), pad(col_geom), vectors, angles)


def in_order(tiles, dim):
    tiles = jnp.moveaxis(tiles, 0, dim)
    shape = tiles.shape
    return tiles.reshape(*shape[:dim], shape[dim] * shape[dim + 1], *shape[dim + 2 :])


def from_everyone(x, axis):
    devices = lax.axis_size(axis)
    return lax.all_to_all(jnp.broadcast_to(x[None], (devices, *x.shape)), axis, 0, 0, tiled=True)


def collect(x, axis, dim):
    return in_order(from_everyone(x, axis), dim)


def cut_along(x, dim, devices):
    shape = x.shape
    tiles = x.reshape(*shape[:dim], devices, shape[dim] // devices, *shape[dim + 1 :])
    return jnp.moveaxis(tiles, dim, 0)


def sent_and_summed(x, axis, dim):
    devices = lax.axis_size(axis)
    tiles = lax.all_to_all(cut_along(x, dim, devices), axis, 0, 0, tiled=True)
    return jnp.sum(tiles, axis=0)


def green_parts(r_sq):
    inverse = lax.rsqrt(r_sq)
    phase = wavenumber * r_sq * inverse
    g_re = jnp.cos(phase) * inverse / four_pi
    g_im = jnp.sin(phase) * inverse / four_pi
    f_re = (-g_re * inverse - wavenumber * g_im) * inverse
    f_im = (-g_im * inverse + wavenumber * g_re) * inverse
    return (g_re, g_im, f_re, f_im)


def incident(geom, blades, harmonic):
    angle = 2.0 * math.pi * jnp.arange(NS, dtype=jnp.float32) / NS
    src_x = cycle_radius * jnp.cos(angle)
    src_y = cycle_radius * jnp.sin(angle)
    dx = geom[0][:, None] - src_x[None, :]
    dy = geom[1][:, None] - src_y[None, :]
    dz = geom[2][:, None] - cycle_height
    r_sq = dx * dx + dy * dy + dz * dz
    g_re, g_im, f_re, f_im = green_parts(r_sq)
    normal_part = (
        dx * geom[3][:, None] + dy * geom[4][:, None] + dz * geom[5][:, None]
    ) / wavenumber
    h_re = g_re - f_im * normal_part
    h_im = g_im + f_re * normal_part
    modes = (blades * harmonic).astype(jnp.float32)
    e_re = jnp.cos(angle[:, None] * modes[None, :])
    e_im = jnp.sin(angle[:, None] * modes[None, :])
    high = lax.Precision.HIGHEST
    b_re = jnp.dot(h_re, e_re, precision=high) - jnp.dot(h_im, e_im, precision=high)
    b_im = jnp.dot(h_re, e_im, precision=high) + jnp.dot(h_im, e_re, precision=high)
    return jnp.concatenate([b_re, b_im], axis=1)


def correction(values, index_local, weights):
    count = index_local.shape[0]
    nvec = values.shape[1] // 2
    nearby = values[index_local]
    w_re = weights[:count][:, :, None]
    w_im = weights[count:][:, :, None]
    part_re = jnp.sum(w_re * nearby[:, :, :nvec] - w_im * nearby[:, :, nvec:], axis=0)
    part_im = jnp.sum(w_re * nearby[:, :, nvec:] + w_im * nearby[:, :, :nvec], axis=0)
    return jnp.concatenate([part_re, part_im], axis=1)


def local(krylov, geometry, corr_index, corr_weight, blades, harmonic, observer_angles):
    nrows = lax.axis_size("rows")
    ncols = lax.axis_size("cols")
    row_at = lax.axis_index("rows")
    col_at = lax.axis_index("cols")
    piece = krylov.shape[0]
    width = krylov.shape[1]
    panels = piece * nrows * ncols
    row_geom = collect(geometry, "cols", 1)
    col_geom = collect(geometry, "rows", 1)
    col_vectors = collect(krylov, "rows", 0)
    obs_each = observer_angles.shape[1] // (nrows * ncols)
    group = ncols * obs_each
    angles = lax.dynamic_slice_in_dim(observer_angles, row_at * group, group, 1)
    part, far_part = tile_products(
        row_geom, col_geom, col_vectors, angles, col_at * piece, row_at * piece, panels
    )
    applied = sent_and_summed(part, "cols", 0)
    first_panel = (row_at * ncols + col_at) * piece
    values = krylov.astype(jnp.float32)
    near = correction(values, corr_index - first_panel, corr_weight)
    source = incident(geometry, blades, harmonic)
    residual = source - (0.5 * values + near + applied)
    far_field = sent_and_summed(far_part, "cols", 0)
    return (residual, far_field)


def solution(mesh):
    placed = (
        P(("rows", "cols"), None),
        P(None, ("rows", "cols")),
        P(None, ("rows", "cols")),
        P(None, ("rows", "cols")),
        P(),
        P(),
        P(),
    )
    return jax.shard_map(
        local,
        mesh=mesh,
        in_specs=placed,
        out_specs=(P(("rows", "cols"), None), P(("rows", "cols"), None)),
        check_vma=False,
    )
```

time: 533 us -> 165 us (0.31); the launches traced: 526 us -> 164 us
  other arithmetic: 406 us -> 3.95 us
  Pallas kernels: 0 us -> 48.5 us
  waiting for transfers between devices: 21.6 us -> 53 us
  blocking collectives: 0 us -> 27.6 us
  loops' own time: 21.9 us -> 0 us
  matrix products: 23.4 us -> 2.88 us
  starting transfers between devices: 30.9 us -> 11.9 us
  local copies, waits for them, and re-layouts: 20.7 us -> 15.1 us
    dot_general x18 -> x0, other arithmetic: 395 us -> none  [the longest x9 197 us: apply_tile(): first = jnp.dot(t_re, vectors, preferred_element_type=jnp.float32)]
    pallas_call x0 -> x1, Pallas kernels: none -> 48.5 us  [tile_products(): pl.pallas_call(body, out_shape=(jax.ShapeDtypeStruct((n_rows, 256), F32),...]
    all_to_all x0 -> x2, blocking collectives: none -> 27.6 us  [from_everyone(): lax.all_to_all(jnp.broadcast_to(x[None], (devices, *x.shape)), axis, 0, 0...]
    another operation x1 -> x0, loops' own time: 21.9 us -> none  [local(): lax.map(one_block, jnp.arange(piece * lax.axis_size('cols') // block, dty...]
    dot_general x18 -> x0, matrix products: 20.5 us -> none  [the longest x9 11.4 us: apply_tile(): second = jnp.dot(t_im, vectors, preferred_element_type=jnp.float32)]
    all_to_all x3 -> x1, waiting for transfers between devices: 4.38 us -> 24.3 us  [from_everyone(): lax.all_to_all(jnp.broadcast_to(x[None], (devices, *x.shape)), axis, 0, 0...]
    all_to_all x3 -> x1, starting transfers between devices: 18.3 us -> 3.95 us  [from_everyone(): lax.all_to_all(jnp.broadcast_to(x[None], (devices, *x.shape)), axis, 0, 0...]
    all_to_all x2, waiting for transfers between devices: 17.2 us -> 28.7 us  [sent_and_summed(): tiles = lax.all_to_all(cut_along(x, dim, devices), axis, 0, 0, tiled=True)]
  transfers between devices with their start and end apart: 5 -> 3, of which waited for: 3 -> 3; matrix products, arithmetic and copies ran while one was open for 84% -> 9% of each run, Pallas kernels for 0% -> 0%
where the time goes in v1:
time: 165 us; the launch traced here: 164 us
  waiting for transfers between devices  53 us (32%)
  Pallas kernels  48.5 us (29%)
  blocking collectives  27.6 us (17%)
  local copies, waits for them, and re-layouts  15.1 us (9%)
  starting transfers between devices  11.9 us (7%)
  other arithmetic  3.95 us (2%)
  matrix products  2.88 us (2%)
    pallas_call x1, Pallas kernels, tile_products(): pl.pallas_call(body, out_shape=(jax.ShapeDtypeStruct((n_rows, 256), F32),...  48.5 us
    all_to_all x2, waiting for transfers between devices, sent_and_summed(): tiles = lax.all_to_all(cut_along(x, dim, devices), axis, 0, 0, tiled=True)  28.7 us
    all_to_all x2, blocking collectives, from_everyone(): lax.all_to_all(jnp.broadcast_to(x[None], (devices, *x.shape)), axis, 0, 0...  27.6 us
    all_to_all x1, waiting for transfers between devices, from_everyone(): lax.all_to_all(jnp.broadcast_to(x[None], (devices, *x.shape)), axis, 0, 0...  24.3 us
    all_to_all x2, starting transfers between devices, sent_and_summed(): tiles = lax.all_to_all(cut_along(x, dim, devices), axis, 0, 0, tiled=True)  7.96 us
    gather x1, local copies, waits for them, and re-layouts, correction(): nearby = values[index_local]  6.64 us
    all_to_all x1, starting transfers between devices, from_everyone(): lax.all_to_all(jnp.broadcast_to(x[None], (devices, *x.shape)), axis, 0, 0...  3.95 us
    broadcast_in_dim x3, local copies, waits for them, and re-layouts, from_everyone(): jnp.broadcast_to(x[None], (devices, *x.shape))  3.9 us
  transfers between devices with their start and end apart: 3, of which 3 were waited for; matrix products, arithmetic and copies ran while one was open for 9% of the time, Pallas kernels for 0%

profile of v1, /device:TPU:1, one launch (start us, length us, event | category | flops | bytes accessed | tf_op | source)
XLA Modules:
  0.0 163.9 jit_solution(13671491988136105901)
XLA Ops:
  0.6 0.0 copy-start
  0.6 0.7 broadcast_in_dim.9
  1.4 14.8 %all_to_all.25 = f32[8,7,256]{2,1,0:T(8,128)S(1)} all-to-all(f32[8,7,256]{2,1,0:T(8,128)S(1)} %broadcast_in_dim.9), channel_id=1, replica_groups=mesh['rows'=16,'cols'=8] {'cols'}, dimensions={0} | all-to-all | bytes 114688 | tf_op jit(solution)/shard_map/all_to_all | solution.py:260
  16.2 0.7 broadcast_in_dim.10
  16.9 12.8 %all_to_all.26 = f32[16,7,256]{2,1,0:T(8,128)S(1)} all-to-all(f32[16,7,256]{2,1,0:T(8,128)S(1)} %broadcast_in_dim.10), channel_id=1, replica_groups=mesh['rows'=16,'cols'=8] {'rows'}, dimensions={0} | all-to-all | bytes 229376 | tf_op jit(solution)/shard_map/all_to_all | solution.py:260
  29.7 2.5 %broadcast_in_dim.11 = bf16[16,256,256]{2,1,0:T(8,128)(2,1)} broadcast(bf16[256,256]{1,0:T(8,128)(2,1)} %param.7), dimensions={1,2} | broadcast | bytes 2228224 | tf_op jit(solution)/shard_map/broadcast_in_dim | solution.py:260
  32.2 4.0 %all-to-all-start.2 = ((bf16[16,256,256]{2,1,0:T(8,128)(2,1)}), bf16[16,256,256]{2,1,0:T(8,128)(2,1)S(1)}, u32[]{:S(2)}, u32[]{:S(2)}) async-start(bf16[16,256,256]{2,1,0:T(8,128)(2,1)} %broadcast_in_dim.11), calls=%async_computation.2 | async-start | bytes 4194304 | tf_op jit(solution)/shard_map/all_to_all | solution.py:260
  36.1 0.0 copy-start.5
  36.1 0.0 copy-start.4
  36.1 0.7 pad_add_fusion.own_ref
  36.8 0.0 copy-done
  36.8 0.6 constant_dynamic-slice_fusion.an
  37.4 0.6 concatenate.14.rg
  38.0 0.7 concatenate.15.cg
  38.7 24.3 %all-to-all-done.2 = bf16[16,256,256]{2,1,0:T(8,128)(2,1)S(1)} async-done(((bf16[16,256,256]{2,1,0:T(8,128)(2,1)}), bf16[16,256,256]{2,1,0:T(8,128)(2,1)S(1)}, u32[]{:S(2)}, u32[]{:S(2)}) %all-to-all-start.2) | async-done | bytes 2097184 | tf_op jit(solution)/shard_map/all_to_all | solution.py:260
  63.0 0.0 copy-start.1
  63.0 1.3 copy-done.1
  64.3 48.5 %tile_products.1 = (f32[2048,256]{1,0:T(8,128)}, f32[512,256]{1,0:T(8,128)}) custom-call(s32[2]{0:T(128)} %pad_add_fusion.own_ref, f32[8,2048]{1,0:T(8,128)} %concatenate.14.rg, f32[8,4096]{1,0:T(8,128)} %concatenate.15.cg, bf16[4096,256]{1,0:T(8,128)(2,1)} %bitcast.22, f32[2,512]{1,0:T(2,128)} %constant_dynamic-slice_fusion.an), custom_call_target="tpu_custom_call" | custom-call | tf_op jit(solution)/shard_map/tile_products/pallas_call | solution.py:236
  112.8 3.5 %all-to-all-start.4 = ((f32[8,64,256]{2,1,0:T(8,128)}), f32[8,64,256]{2,1,0:T(8,128)S(1)}, u32[]{:S(2)}, u32[]{:S(2)}) async-start(f32[8,64,256]{2,1,0:T(8,128)} %bitcast.24), calls=%async_computation.4 | async-start | bytes 1048576 | tf_op jit(solution)/shard_map/all_to_all | solution.py:275
  116.3 0.0 copy-done.5
  116.4 0.0 copy-done.4
  116.4 11.6 %all-to-all-done.4 = f32[8,64,256]{2,1,0:T(8,128)S(1)} async-done(((f32[8,64,256]{2,1,0:T(8,128)}), f32[8,64,256]{2,1,0:T(8,128)S(1)}, u32[]{:S(2)}, u32[]{:S(2)}) %all-to-all-start.4) | async-done | bytes 524320 | tf_op jit(solution)/shard_map/all_to_all | solution.py:275
  128.0 0.0 copy-start.2
  128.0 4.5 %all-to-all-start.3 = ((f32[8,256,256]{2,1,0:T(8,128)}), f32[8,256,256]{2,1,0:T(8,128)}, u32[]{:S(2)}, u32[]{:S(2)}) async-start(f32[8,256,256]{2,1,0:T(8,128)} %bitcast.23), calls=%async_computation.3 | async-start | bytes 4194304 | tf_op jit(solution)/shard_map/all_to_all | solution.py:275
  132.5 0.0 copy-done.2
  132.5 0.1 copy.18
  132.6 0.1 copy.19
  132.7 6.6 %gather_fusion = f32[2048,256]{1,0:T(8,128)S(1)} fusion(f32[256,256]{1,0:T(8,128)S(1)} %copy.19, s32[2048]{0:T(1024)S(1)} %broadcast_clamp_fusion), kind=kCustom, calls=%fused_computation | custom fusion | bytes 4202496 | tf_op jit(solution)/shard_map/gather | solution.py:315
  139.4 0.0 copy-start.6
  139.4 0.0 copy-start.7
  139.4 0.0 copy-start.3
  139.4 0.7 subtract_reduce_fusion
  140.2 0.1 copy.20
  140.3 0.1 copy.21
  140.4 0.0 copy-done.6
  140.4 0.0 copy-done.7
  140.5 0.0 copy-done.3
  140.5 0.7 fusion.21
  141.2 0.7 fusion.22
  141.9 0.7 convolution_subtract_fusion
  142.7 0.7 convolution_add_fusion
  143.4 0.7 reduce_sum.39
  144.1 17.1 %all-to-all-done.3 = f32[8,256,256]{2,1,0:T(8,128)} async-done(((f32[8,256,256]{2,1,0:T(8,128)}), f32[8,256,256]{2,1,0:T(8,128)}, u32[]{:S(2)}, u32[]{:S(2)}) %all-to-all-start.3) | async-done | bytes 2097184 | tf_op jit(solution)/shard_map/all_to_all | solution.py:275
  161.1 1.8 %reduce_sum.38 = f32[256,256]{1,0:T(8,128)S(1)} reduce(f32[8,256,256]{2,1,0:T(8,128)} %all-to-all-done.3, f32[]{:T(128)} %constant.45.clone.1), dimensions={0}, to_apply=%region_2.0 | reduce | flops 458752 | bytes 2359300 | tf_op jit(solution)/shard_map/reduce_sum | solution.py:276
  162.9 0.1 copy.22
  163.0 0.1 maximum_subtract_fusion
  163.1 0.8 copy.23
  (8 shorter events, 0.1 us)
Async XLA Ops:
  0.6 36.2 %copy-start = (f32[2,8192]{1,0:T(2,128)S(1)}, f32[2,8192]{1,0:T(2,128)}, u32[]{:S(2)}) copy-start(f32[2,8192]{1,0:T(2,128)} %param.13) | copy-start | bytes 196612
  32.2 30.9 %all-to-all-start.2 = ((bf16[16,256,256]{2,1,0:T(8,128)(2,1)}), bf16[16,256,256]{2,1,0:T(8,128)(2,1)S(1)}, u32[]{:S(2)}, u32[]{:S(2)}) async-start(bf16[16,256,256]{2,1,0:T(8,128)(2,1)} %broadcast_in_dim.11), calls=%async_computation.2 | async-start | bytes 4194304 | tf_op jit(solution)/shard_map/all_to_all | solution.py:260
  36.1 80.2 %copy-start.5 = (s32[8,256]{1,0:T(8,128)S(1)}, s32[8,256]{1,0:T(8,128)}, u32[]{:S(2)}) copy-start(s32[8,256]{1,0:T(8,128)} %param.9) | copy-start | bytes 24580
  36.1 80.3 %copy-start.4 = (f32[16,256]{1,0:T(8,128)S(1)}, f32[16,256]{1,0:T(8,128)}, u32[]{:S(2)}) copy-start(f32[16,256]{1,0:T(8,128)} %param.10) | copy-start | bytes 49156
  63.0 1.3 copy-start.1
  112.8 15.2 %all-to-all-start.4 = ((f32[8,64,256]{2,1,0:T(8,128)}), f32[8,64,256]{2,1,0:T(8,128)S(1)}, u32[]{:S(2)}, u32[]{:S(2)}) async-start(f32[8,64,256]{2,1,0:T(8,128)} %bitcast.24), calls=%async_computation.4 | async-start | bytes 1048576 | tf_op jit(solution)/shard_map/all_to_all | solution.py:275
  128.0 4.5 %copy-start.2 = (bf16[256,256]{1,0:T(8,128)(2,1)S(1)}, bf16[256,256]{1,0:T(8,128)(2,1)}, u32[]{:S(2)}) copy-start(bf16[256,256]{1,0:T(8,128)(2,1)} %param.7) | copy-start | bytes 393220
  128.0 33.1 %all-to-all-start.3 = ((f32[8,256,256]{2,1,0:T(8,128)}), f32[8,256,256]{2,1,0:T(8,128)}, u32[]{:S(2)}, u32[]{:S(2)}) async-start(f32[8,256,256]{2,1,0:T(8,128)} %bitcast.23), calls=%async_computation.3 | async-start | bytes 4194304 | tf_op jit(solution)/shard_map/all_to_all | solution.py:275
  139.4 1.0 copy-start.6
  139.4 1.0 copy-start.7
  139.4 1.0 copy-start.3

commit v2 on v1

v2 whole, which is shorter than its diff:
```python
import functools
import math

import jax
import jax.numpy as jnp
from jax import lax
from jax.experimental import pallas as pl
from jax.experimental.pallas import tpu as pltpu
from jax.sharding import PartitionSpec as P

BF = jnp.bfloat16
F32 = jnp.float32
NS = 64
LANES = 128

wavenumber = 20.0
cycle_radius = 0.7
cycle_height = 1.0
four_pi = 4.0 * math.pi
two_pi = 2.0 * math.pi
kappa = wavenumber / two_pi

dot = functools.partial(jnp.dot, preferred_element_type=F32)


def pieces(x):
    first = x.astype(BF).astype(F32)
    rest = x - first
    second = rest.astype(BF).astype(F32)
    return first, second, (rest - second).astype(BF).astype(F32)


def left_stack(x):
    a, b, c = pieces(x)
    return jnp.concatenate([a, a, b, a, c, b], axis=0)


def right_stack(x):
    a, b, c = pieces(x)
    return jnp.concatenate([a, b, a, c, a, b], axis=0).astype(BF)


def panel_rows(g):
    row = lax.broadcasted_iota(jnp.int32, g.shape, 0)
    center = row < 3
    normal = pltpu.roll(g, 5, 0)
    c_sq = jnp.sum(jnp.where(center, g * g, 0.0), axis=0, keepdims=True)
    n_c = jnp.sum(jnp.where(center, g * normal, 0.0), axis=0, keepdims=True)
    return row, center, normal, c_sq, n_c, g[6:7]


def left_features(g, soft_sq):
    row, center, normal, c_sq, n_c, _ = panel_rows(g)
    size = (kappa * kappa) * (c_sq + soft_sq)
    one = jnp.where(row == 3, 1.0, jnp.where(row == 4, size, 0.0))
    two = jnp.where(row == 3, n_c, 0.0)
    return (
        left_stack(jnp.where(center, g, one)),
        left_stack(jnp.where(center, normal, two)),
    )


def right_features(g):
    row, center, normal, c_sq, n_c, area = panel_rows(g)
    scale = area * (kappa * kappa / four_pi)
    k_sq = kappa * kappa
    r_sq = jnp.where(
        center, -2.0 * k_sq * g, jnp.where(row == 3, k_sq * c_sq, jnp.where(row == 4, 1.0, 0.0))
    )
    along_col = jnp.where(
        center, -wavenumber * scale * normal, jnp.where(row == 3, wavenumber * scale * n_c, 0.0)
    )
    along_row = jnp.where(center, scale * g, jnp.where(row == 3, -scale, 0.0))
    far_turns = jnp.where(center, kappa * g, 0.0)
    far_scale = jnp.where(center, -wavenumber * area * normal, 0.0)
    return [right_stack(v) for v in (r_sq, along_col, along_row, far_turns, far_scale)]


def operator_tile(r_sq, along_col, along_row):
    inv = lax.rsqrt(r_sq)
    turns = r_sq * inv
    part = (turns - jnp.round(turns)).astype(BF)
    u = inv.astype(BF)
    a = along_col.astype(BF)
    b = along_row.astype(BF)

    def const(v):
        return jnp.asarray(v, BF)

    z = part * part
    sin_poly = (z * const(SIN[2]) + const(SIN[1])) * z + const(SIN[0])
    cos_poly = (z * const(COS[2]) + const(COS[1])) * z + const(COS[0])
    s = (part * u) * sin_poly
    c = u * cos_poly
    re = u * u - s * s
    im = s * c
    w = u * const(1.0 / two_pi)
    p = b - w * a
    q = a + w * b
    return re * p - im * q, re * q + im * p


root2 = math.sqrt(2.0)
SIN = [root2 * v for v in (3.14064003, -5.1369052, 2.29954689)]
COS = [root2 * v for v in (0.99940322, -4.89118661, 3.5838431)]


def far_values(turns, scale):
    part = turns - jnp.round(turns)
    z = part * part
    s = part * (((z * -0.55463616 + 2.54189901) * z + -5.16714279) * z + 3.14158202)
    c = ((z * -1.22212692 + 4.04128377) * z + -4.93393801) * z + 0.9999933
    s2 = s + s
    return (scale * (s2 * c)).astype(BF), (scale * (1.0 - s2 * s)).astype(BF)


def sin_cos(turns):
    part = turns - jnp.round(turns)
    quarter = jnp.round(4.0 * part)
    y = (part - 0.25 * quarter) * two_pi
    z = y * y
    s = y * (1.0 + z * (-1.0 / 6 + z * (1.0 / 120 + z * (-1.0 / 5040 + z * (1.0 / 362880)))))
    c = 1.0 + z * (-0.5 + z * (1.0 / 24 + z * (-1.0 / 720 + z * (1.0 / 40320))))
    odd = jnp.abs(quarter) == 1.0
    sin_v = jnp.where(odd, c, s)
    cos_v = jnp.where(odd, s, c)
    sin_v = jnp.where((quarter == -1.0) | (jnp.abs(quarter) == 2.0), -sin_v, sin_v)
    cos_v = jnp.where((quarter == 1.0) | (jnp.abs(quarter) == 2.0), -cos_v, cos_v)
    return sin_v, cos_v


ROWS = 512
COLS = 512
BLOCK = 256
MESH = pl.DeviceIdType.MESH


def turned(x):
    half = x.shape[1] // 2
    return jnp.concatenate([-x[:, half:], x[:, :half]], axis=1)


def incident(g, blades, harmonic):
    gt = g.T
    col = lambda i: gt[:, i : i + 1]
    source = lax.broadcasted_iota(jnp.int32, (1, NS), 1).astype(F32) * (1.0 / NS)
    sin_s, cos_s = sin_cos(source)
    dx = col(0) - cycle_radius * cos_s
    dy = col(1) - cycle_radius * sin_s
    dz = col(2) - cycle_height
    r_sq = dx * dx + dy * dy + dz * dz
    inv = lax.rsqrt(r_sq)
    sin_r, cos_r = sin_cos(r_sq * inv * kappa)
    g_re = cos_r * inv * (1.0 / four_pi)
    g_im = sin_r * inv * (1.0 / four_pi)
    f_re = (-g_re * inv - wavenumber * g_im) * inv
    f_im = (-g_im * inv + wavenumber * g_re) * inv
    along = (dx * col(3) + dy * col(4) + dz * col(5)) * (1.0 / wavenumber)
    h = jnp.concatenate([g_re - f_im * along, g_im + f_re * along], axis=1)
    modes = blades * harmonic
    at = lax.broadcasted_iota(jnp.int32, (NS, modes.shape[1]), 0)
    e_im, e_re = sin_cos(((at * modes) % NS).astype(F32) * (1.0 / NS))
    e = jnp.concatenate(
        [jnp.concatenate([e_re, e_im], axis=1), jnp.concatenate([-e_im, e_re], axis=1)], axis=0
    )
    return jnp.dot(h, e, precision=lax.Precision.HIGHEST, preferred_element_type=F32)


def correction(x, index, weight):
    count, n = index.shape
    both = jnp.concatenate([index.astype(F32), weight], axis=0).T
    lane = lax.broadcasted_iota(jnp.int32, (n, n), 1).astype(F32)
    w_re = jnp.zeros((n, n), F32)
    w_im = jnp.zeros((n, n), F32)
    for c in range(count):
        hit = lane == both[:, c : c + 1]
        w_re += jnp.where(hit, both[:, count + c : count + c + 1], 0.0)
        w_im += jnp.where(hit, both[:, 2 * count + c : 2 * count + c + 1], 0.0)
    x2 = jnp.concatenate([x, turned(x)], axis=0)
    total = jnp.zeros((n, x.shape[1]), F32)
    for part in pieces(jnp.concatenate([w_re, w_im], axis=1)):
        total += dot(part.astype(BF), x2)
    return total


def kernel(
    nrows, ncols,
    krylov, geometry, corr_index, corr_weight, blades, harmonic, angles,
    out, far_out,
    cgeo, rgeo, left_a, left_b, r0, r1, r2, r3, r4, x2, p0, p1, p2, p3, p4, p5, t0, t1, acc, base,
    stage, far_stage, part_in, far_in,
    send_sem, cgeo_sem, rgeo_sem, x_sem, far_sem, part_sem,
):
    rights = (r0, r1, r2, r3, r4)
    planes = ((p0, p1, p2), (p3, p4, p5))
    tiles = (t0, t1)
    r = lax.axis_index("rows")
    c = lax.axis_index("cols")
    core = r % 2
    chip = r // 2
    chips = nrows // 2
    sibling = r + 1 - 2 * core
    n_cols = nrows * BLOCK
    n_rows = ncols * BLOCK
    n_obs = far_stage.shape[0]
    obs = n_obs // ncols
    steps = n_cols // COLS
    half = COLS // LANES
    panels = nrows * ncols * BLOCK
    sends = []

    def send(src, dst, sem, row, col):
        copy = pltpu.make_async_remote_copy(
            src_ref=src, dst_ref=dst, send_sem=send_sem.at[len(sends)], recv_sem=sem,
            device_id=(row, col), device_id_type=MESH,
        )
        copy.start()
        sends.append(copy)

    def arrived(dst, sem):
        pltpu.make_async_remote_copy(
            src_ref=dst, dst_ref=dst, send_sem=send_sem.at[0], recv_sem=sem,
            device_id=(r, c), device_id_type=MESH,
        ).wait_recv()

    barrier = pltpu.get_barrier_semaphore()
    for k in range(1, nrows):
        pl.semaphore_signal(barrier, inc=1, device_id=((r + k) % nrows, c), device_id_type=MESH)
    for k in range(1, ncols):
        pl.semaphore_signal(barrier, inc=1, device_id=(r, (c + k) % ncols), device_id_type=MESH)

    ang = angles[:, pl.ds(pl.multiple_of(r * n_obs, n_obs), n_obs)] * (1.0 / two_pi)
    sin_t, cos_t = sin_cos(ang[0:1])
    sin_p, cos_p = sin_cos(ang[1:2])
    e = jnp.concatenate([sin_t * cos_p, sin_t * sin_p, cos_t, jnp.zeros((5, n_obs), F32)], axis=0)
    left_a[pl.ds(n_rows, n_obs), :] = left_stack(e).T.astype(BF)
    cgeo[chip] = geometry[...]
    rgeo[c] = geometry[...]
    x2[chip // 2, chip % 2] = krylov[...]

    pl.semaphore_wait(barrier, nrows + ncols - 2)
    for k in range(1, nrows):
        peer = (r + k) % nrows
        at = (r + peer) % 2 * chips + chip
        send(geometry, cgeo.at[at], cgeo_sem.at[at], peer, c)
    for k in range(1, ncols):
        send(geometry, rgeo.at[c], rgeo_sem.at[c], r, (c + k) % ncols)
    send(krylov, x2.at[(chips + chip) // 2, chip % 2], x_sem.at[chips + chip], sibling, c)
    for k in range(1, chips):
        peer = (chip + k) % chips * 2 + core
        send(krylov, x2.at[chip // 2, chip % 2], x_sem.at[chip], peer, c)

    own = jnp.concatenate([geometry[...], jnp.zeros((1, BLOCK), F32)], axis=0)
    x = krylov[...]
    index = corr_index[...] - (r * ncols + c) * BLOCK
    base[...] = (
        incident(own, blades[...], harmonic[...])
        - 0.5 * x.astype(F32)
        - correction(x, index, corr_weight[...])
    )

    for k in range(1, nrows):
        at = (chip + k) % nrows
        arrived(cgeo.at[at], cgeo_sem.at[at])
    g = jnp.concatenate([cgeo[i] for i in range(nrows)], axis=1)
    g = jnp.concatenate([g, jnp.zeros((1, n_cols), F32)], axis=0)
    for ref, v in zip(rights, right_features(g)):
        ref[...] = v
    for k in range(1, ncols):
        at = (c + k) % ncols
        arrived(rgeo.at[at], rgeo_sem.at[at])
    g = jnp.concatenate([rgeo[i] for i in range(ncols)], axis=1)
    g = jnp.concatenate([g, jnp.zeros((1, n_rows), F32)], axis=0)
    la, lb = left_features(g, 4.0 / panels)
    left_a[pl.ds(0, n_rows), :] = la.T.astype(BF)
    left_b[...] = lb.T.astype(BF)

    def make_geometry(first, step, far, into):
        cols = pl.ds(pl.multiple_of(step * COLS, COLS), COLS)
        rows = pl.ds(pl.multiple_of(first, ROWS), ROWS)
        la = left_a[rows, :]
        if far:
            into[0][...] = dot(la, rights[3][:, cols])
            into[1][...] = dot(la, rights[4][:, cols])
        else:
            into[0][...] = dot(la, rights[0][:, cols])
            into[1][...] = dot(la, rights[1][:, cols])
            into[2][...] = dot(left_b[rows, :], rights[2][:, cols])

    def make_values(step, far, frm, tile):
        if far:
            re, im = far_values(frm[0][...], frm[1][...])
        else:
            re, im = operator_tile(frm[0][...], frm[1][...], frm[2][...])
        for h in range(half):
            tile[step * 2 * half + h] = re[:, h * LANES : (h + 1) * LANES]
            tile[step * 2 * half + half + h] = im[:, h * LANES : (h + 1) * LANES]

    def product(step, tile, rows):
        lhs = jnp.concatenate([tile[step * 2 * half + h, rows, :] for h in range(2 * half)], axis=1)
        return dot(lhs, x2[step].reshape(2 * COLS, x2.shape[-1]))

    every = pl.ds(0, ROWS)
    blocks = n_rows // ROWS
    where = [(c // 2 + 1 + b) % blocks for b in range(blocks)]
    seq = [(n_rows, True)] + [(w * ROWS, False) for w in where]

    def run(ph, first_h, last_h, prepare):
        gen, mul = ph < len(seq), ph > 0

        @pl.loop(first_h, last_h)
        def _(h):
            for par in range(2):
                step = 2 * h + par
                if gen:
                    first, far = seq[ph]
                    make_geometry(first, lax.rem(step + 1, steps), far, planes[1 - par])
                    make_values(step, far, planes[par], tiles[ph % 2])
                if mul:
                    if prepare:
                        for b in range(2):
                            if prepare > 1:
                                arrived(x2.at[step, b], x_sem.at[2 * step + b])
                            x2[step, 2 + b] = turned(x2[step, b])
                    acc[...] += product(step, tiles[(ph - 1) % 2], every)

    def send_parts(block):
        for b in range(2):
            owner = where[block] * 2 + b
            send(stage.at[owner], part_in.at[c], part_sem.at[c], r, owner)

    for ph in range(len(seq)):
        first, far = seq[ph]
        make_geometry(first, 0, far, planes[0])
        if ph > 0:
            acc[...] = jnp.zeros_like(acc)
        if ph == 2:
            for k in range(1, ncols):
                owner = (c + k) % ncols
                rows = pl.ds(pl.multiple_of(owner * obs, obs), obs)
                send(far_stage.at[rows, :], far_in.at[c], far_sem.at[c], r, owner)
        if ph > 2:
            send_parts(ph - 3)
        if ph == 1:
            run(ph, 0, steps // 4, 1)
            run(ph, steps // 4, steps // 2, 2)
        else:
            run(ph, 0, steps // 2, 0)
        if ph == 0:
            for k in range(1, chips):
                at = (chip + k) % chips
                here = x2.at[at // 2, at % 2]
                arrived(here, x_sem.at[at])
                send(here, x2.at[(chips + at) // 2, at % 2], x_sem.at[chips + at], sibling, c)
        elif ph == 1:
            far_stage[...] = acc[...]
        else:
            for b in range(2):
                stage[where[ph - 2] * 2 + b] = acc[pl.ds(b * BLOCK, BLOCK), :].astype(BF)

    tile = tiles[(len(seq) - 1) % 2]
    same = lax.broadcasted_iota(jnp.int32, (BLOCK, LANES), 0)
    lane = lax.broadcasted_iota(jnp.int32, (BLOCK, LANES), 1)
    rows = pl.ds(pl.multiple_of(c % 2 * BLOCK, BLOCK), BLOCK)
    for h in range(BLOCK // LANES):
        for part in range(2):
            at = chip // 2 * 2 * half + part * half + chip % 2 * (BLOCK // LANES) + h
            v = tile[at, rows, :].astype(F32)
            tile[at, rows, :] = jnp.where(same == lane + h * LANES, 0.0, v).astype(BF)

    send_parts(blocks - 2)
    partner = c + 1 - 2 * (c % 2)
    mine = acc.at[pl.ds(0, BLOCK), :]
    theirs = acc.at[pl.ds(BLOCK, BLOCK), :]
    other_rows = pl.ds(pl.multiple_of((1 - c % 2) * BLOCK, BLOCK), BLOCK)
    theirs[...] = product(0, tile, other_rows)

    @pl.loop(1, steps)
    def _(step):
        theirs[...] += product(step, tile, other_rows)

    stage[partner] = theirs[...].astype(BF)
    mine[...] = product(0, tile, rows)
    send(stage.at[partner], part_in.at[c], part_sem.at[c], r, partner)

    @pl.loop(1, steps)
    def _(step):
        mine[...] += product(step, tile, rows)

    total = far_stage[pl.ds(pl.multiple_of(c * obs, obs), obs), :]
    for k in range(1, ncols):
        at = (c + k) % ncols
        arrived(far_in.at[at], far_sem.at[at])
        total += far_in[at]
    far_out[...] = total
    total = base[...] - mine[...]
    for k in range(1, ncols):
        at = (c + k) % ncols
        arrived(part_in.at[at], part_sem.at[at])
        total -= part_in[at].astype(F32)
    out[...] = total
    for copy in sends:
        copy.wait_send()


def local(krylov, geometry, corr_index, corr_weight, blades, harmonic, observer_angles):
    nrows = lax.axis_size("rows")
    ncols = lax.axis_size("cols")
    width = krylov.shape[1]
    n_cols, n_rows = nrows * BLOCK, ncols * BLOCK
    n_obs = observer_angles.shape[1] // nrows
    n_sends = (nrows - 1) + 4 * (ncols - 1) + nrows
    vm = pl.BlockSpec(memory_space=pltpu.VMEM)
    dma = pltpu.SemaphoreType.DMA
    return pl.pallas_call(
        functools.partial(kernel, nrows, ncols),
        out_shape=(
            jax.ShapeDtypeStruct((BLOCK, width), F32),
            jax.ShapeDtypeStruct((n_obs // ncols, width), F32),
        ),
        in_specs=[vm] * 7,
        out_specs=(vm, vm),
        scratch_shapes=[
            pltpu.VMEM((nrows, 7, BLOCK), F32),
            pltpu.VMEM((ncols, 7, BLOCK), F32),
            pltpu.VMEM((n_rows + n_obs, 48), BF),
            pltpu.VMEM((n_rows, 48), BF),
        ]
        + [pltpu.VMEM((48, n_cols), BF)] * 5
        + [pltpu.VMEM((n_cols // COLS, 4, BLOCK, width), BF)]
        + [pltpu.VMEM((ROWS, COLS), F32)] * 6
        + [pltpu.VMEM((2 * n_cols // LANES, ROWS, LANES), BF)] * 2
        + [
            pltpu.VMEM((ROWS, width), F32),
            pltpu.VMEM((BLOCK, width), F32),
            pltpu.VMEM((ncols, BLOCK, width), BF),
            pltpu.VMEM((n_obs, width), F32),
            pltpu.VMEM((ncols, BLOCK, width), BF),
            pltpu.VMEM((ncols, n_obs // ncols, width), F32),
            dma((n_sends,)),
            dma((nrows,)),
            dma((ncols,)),
            dma((nrows,)),
            dma((ncols,)),
            dma((ncols,)),
        ],
        compiler_params=pltpu.CompilerParams(
            collective_id=0, has_side_effects=True, vmem_limit_bytes=60 << 20
        ),
        name="burton_miller",
    )(krylov, geometry, corr_index, corr_weight, blades[None], harmonic[None], observer_angles)


def solution(mesh):
    placed = (
        P(("rows", "cols"), None),
        P(None, ("rows", "cols")),
        P(None, ("rows", "cols")),
        P(None, ("rows", "cols")),
        P(),
        P(),
        P(),
    )
    return jax.shard_map(
        local,
        mesh=mesh,
        in_specs=placed,
        out_specs=(P(("rows", "cols"), None), P(("rows", "cols"), None)),
        check_vma=False,
    )
```

time: 165 us -> 81.7 us (0.50)
  the two profiles are of different devices: /device:TPU:1 before, /device:TPU:26 now
where the time goes in v2:
time: 81.7 us; the launch traced here: 81.6 us
  Pallas kernels  78.6 us (96%)
  local copies, waits for them, and re-layouts  2.33 us (3%)
    pallas_call x1, Pallas kernels, local(): pl.pallas_call(functools.partial(kernel, nrows, ncols), out_shape=(jax.Sh...  78.6 us
    unnamed x4, local copies, waits for them, and re-layouts  2.33 us

profile of v2, /device:TPU:26, one launch (start us, length us, event | category | flops | bytes accessed | tf_op | source)
XLA Modules:
  0.0 81.6 jit_solution(14018423031089237492)
XLA Ops:
  0.6 78.6 %burton_miller.1 = (f32[256,256]{1,0:T(8,128)}, f32[64,256]{1,0:T(8,128)}) custom-call(bf16[256,256]{1,0:T(8,128)(2,1)} %krylov.1, f32[7,256]{1,0:T(8,128)} %geometry.1, s32[8,256]{1,0:T(8,128)} %corr_index.1, f32[16,256]{1,0:T(8,128)} %corr_weight.1, s32[1,128]{1,0:T(1,128)} %bitcast.2, s32[1,128]{1,0:T(1,128)} %bitcast.3, f32[2,8192]{1,0:T(2,128)} %angles.1), custom_call_target="tpu_custom_call" | custom-call | tf_op jit(solution)/shard_map/burton_miller/pallas_call | solution.py:415
  79.2 0.0 copy-start
  79.2 1.7 %copy.11 = f32[256,256]{1,0:T(8,128)} copy(f32[256,256]{1,0:T(8,128)} %get-tuple-element.4) | data formatting | bytes 524288
  80.9 0.0 copy-done
  80.9 0.6 copy.12
Async XLA Ops:
  79.2 1.7 %copy-start = (f32[64,256]{1,0:T(8,128)S(1)}, f32[64,256]{1,0:T(8,128)}, u32[]{:S(2)}) copy-start(f32[64,256]{1,0:T(8,128)} %get-tuple-element.5) | copy-start | bytes 196612

commit v3 on v2

--- a/solution.py
+++ b/solution.py
@@ -184,16 +184,16 @@
 
 
 def kernel(
-    nrows, ncols,
+    nrows, ncols, left_a, left_b, r0, r1, r2, r3, r4, t0, t1, t2,
     krylov, geometry, corr_index, corr_weight, blades, harmonic, angles,
     out, far_out,
-    cgeo, rgeo, left_a, left_b, r0, r1, r2, r3, r4, x2, p0, p1, p2, p3, p4, p5, t0, t1, acc, base,
+    cgeo, rgeo, x2, p0, p1, p2, p3, p4, p5, acc, base,
     stage, far_stage, part_in, far_in,
     send_sem, cgeo_sem, rgeo_sem, x_sem, far_sem, part_sem,
 ):
     rights = (r0, r1, r2, r3, r4)
     planes = ((p0, p1, p2), (p3, p4, p5))
-    tiles = (t0, t1)
+    tiles = (t0, t1, t2)
     r = lax.axis_index("rows")
     c = lax.axis_index("cols")
     core = r % 2
@@ -208,6 +208,7 @@
     half = COLS // LANES
     panels = nrows * ncols * BLOCK
     sends = []
+    first_forward = (nrows - 1) + 3 * (ncols - 1) + chips
 
     def send(src, dst, sem, row, col):
         copy = pltpu.make_async_remote_copy(
@@ -216,6 +217,13 @@
         )
         copy.start()
         sends.append(copy)
+
+    def forward(k, at):
+        return pltpu.make_async_remote_copy(
+            src_ref=x2.at[at // 2, at % 2], dst_ref=x2.at[(chips + at) // 2, at % 2],
+            send_sem=send_sem.at[first_forward + k - 1], recv_sem=x_sem.at[chips + at],
+            device_id=(sibling, c), device_id_type=MESH,
+        )
 
     def arrived(dst, sem):
         pltpu.make_async_remote_copy(
@@ -237,6 +245,10 @@
     cgeo[chip] = geometry[...]
     rgeo[c] = geometry[...]
     x2[chip // 2, chip % 2] = krylov[...]
+
+    x = krylov[...]
+    index = corr_index[...] - (r * ncols + c) * BLOCK
+    base[...] = -0.5 * x.astype(F32) - correction(x, index, corr_weight[...])
 
     pl.semaphore_wait(barrier, nrows + ncols - 2)
     for k in range(1, nrows):
@@ -251,13 +263,7 @@
         send(krylov, x2.at[chip // 2, chip % 2], x_sem.at[chip], peer, c)
 
     own = jnp.concatenate([geometry[...], jnp.zeros((1, BLOCK), F32)], axis=0)
-    x = krylov[...]
-    index = corr_index[...] - (r * ncols + c) * BLOCK
-    base[...] = (
-        incident(own, blades[...], harmonic[...])
-        - 0.5 * x.astype(F32)
-        - correction(x, index, corr_weight[...])
-    )
+    base[...] += incident(own, blades[...], harmonic[...])
 
     for k in range(1, nrows):
         at = (chip + k) % nrows
@@ -304,9 +310,14 @@
     blocks = n_rows // ROWS
     where = [(c // 2 + 1 + b) % blocks for b in range(blocks)]
     seq = [(n_rows, True)] + [(w * ROWS, False) for w in where]
-
-    def run(ph, first_h, last_h, prepare):
-        gen, mul = ph < len(seq), ph > 0
+    lag = 2
+
+    def prepare(step):
+        for b in range(2):
+            x2[step, 2 + b] = turned(x2[step, b])
+
+    def run(ph, first_h, last_h, extra=None):
+        gen, mul = ph < len(seq), ph >= lag
 
         @pl.loop(first_h, last_h)
         def _(h):
@@ -315,50 +326,56 @@
                 if gen:
                     first, far = seq[ph]
                     make_geometry(first, lax.rem(step + 1, steps), far, planes[1 - par])
-                    make_values(step, far, planes[par], tiles[ph % 2])
+                    make_values(step, far, planes[par], tiles[ph % 3])
+                if extra is not None:
+                    extra(step)
                 if mul:
-                    if prepare:
-                        for b in range(2):
-                            if prepare > 1:
-                                arrived(x2.at[step, b], x_sem.at[2 * step + b])
-                            x2[step, 2 + b] = turned(x2[step, b])
-                    acc[...] += product(step, tiles[(ph - 1) % 2], every)
+                    acc[...] += product(step, tiles[(ph - lag) % 3], every)
+
+    def pass_on(step):
+        @pl.when(step > 0)
+        def _():
+            at = (chip + chips - step) % chips
+            arrived(x2.at[at // 2, at % 2], x_sem.at[at])
+            forward(step, at).start()
+
+    def wait_and_prepare(step):
+        for b in range(2):
+            arrived(x2.at[step, b], x_sem.at[2 * step + b])
+        prepare(step)
 
     def send_parts(block):
         for b in range(2):
             owner = where[block] * 2 + b
             send(stage.at[owner], part_in.at[c], part_sem.at[c], r, owner)
 
-    for ph in range(len(seq)):
-        first, far = seq[ph]
-        make_geometry(first, 0, far, planes[0])
-        if ph > 0:
+    for ph in range(len(seq) + 1):
+        if ph < len(seq):
+            first, far = seq[ph]
+            make_geometry(first, 0, far, planes[0])
+        if ph >= lag:
             acc[...] = jnp.zeros_like(acc)
-        if ph == 2:
+        if ph == 3:
             for k in range(1, ncols):
                 owner = (c + k) % ncols
                 rows = pl.ds(pl.multiple_of(owner * obs, obs), obs)
                 send(far_stage.at[rows, :], far_in.at[c], far_sem.at[c], r, owner)
-        if ph > 2:
-            send_parts(ph - 3)
+        if ph > 3:
+            send_parts(ph - 4)
         if ph == 1:
-            run(ph, 0, steps // 4, 1)
-            run(ph, steps // 4, steps // 2, 2)
+            run(ph, 0, steps // 2, pass_on)
+        elif ph == 2:
+            run(ph, 0, steps // 4, prepare)
+            run(ph, steps // 4, steps // 2, wait_and_prepare)
         else:
-            run(ph, 0, steps // 2, 0)
-        if ph == 0:
-            for k in range(1, chips):
-                at = (chip + k) % chips
-                here = x2.at[at // 2, at % 2]
-                arrived(here, x_sem.at[at])
-                send(here, x2.at[(chips + at) // 2, at % 2], x_sem.at[chips + at], sibling, c)
-        elif ph == 1:
+            run(ph, 0, steps // 2)
+        if ph == 2:
             far_stage[...] = acc[...]
-        else:
+        elif ph > 2:
             for b in range(2):
-                stage[where[ph - 2] * 2 + b] = acc[pl.ds(b * BLOCK, BLOCK), :].astype(BF)
-
-    tile = tiles[(len(seq) - 1) % 2]
+                stage[where[ph - 3] * 2 + b] = acc[pl.ds(b * BLOCK, BLOCK), :].astype(BF)
+
+    tile = tiles[(len(seq) - 1) % 3]
     same = lax.broadcasted_iota(jnp.int32, (BLOCK, LANES), 0)
     lane = lax.broadcasted_iota(jnp.int32, (BLOCK, LANES), 1)
     rows = pl.ds(pl.multiple_of(c % 2 * BLOCK, BLOCK), BLOCK)
@@ -389,18 +406,20 @@
 
     total = far_stage[pl.ds(pl.multiple_of(c * obs, obs), obs), :]
     for k in range(1, ncols):
-        at = (c + k) % ncols
+        at = (c + ncols - k) % ncols
         arrived(far_in.at[at], far_sem.at[at])
         total += far_in[at]
     far_out[...] = total
     total = base[...] - mine[...]
     for k in range(1, ncols):
-        at = (c + k) % ncols
+        at = (c + ncols - k) % ncols
         arrived(part_in.at[at], part_sem.at[at])
         total -= part_in[at].astype(F32)
     out[...] = total
     for copy in sends:
         copy.wait_send()
+    for k in range(1, chips):
+        forward(k, (chip + chips - k) % chips).wait_send()
 
 
 def local(krylov, geometry, corr_index, corr_weight, blades, harmonic, observer_angles):
@@ -410,10 +429,19 @@
     n_cols, n_rows = nrows * BLOCK, ncols * BLOCK
     n_obs = observer_angles.shape[1] // nrows
     n_sends = (nrows - 1) + 4 * (ncols - 1) + nrows
+    scoped = (
+        [pltpu.VMEM((n_rows + n_obs, 48), BF), pltpu.VMEM((n_rows, 48), BF)]
+        + [pltpu.VMEM((48, n_cols), BF)] * 5
+        + [pltpu.VMEM((2 * n_cols // LANES, ROWS, LANES), BF)] * 3
+    )
+
+    def body(*refs):
+        pl.run_scoped(lambda *own: kernel(nrows, ncols, *own, *refs), *scoped)
+
     vm = pl.BlockSpec(memory_space=pltpu.VMEM)
     dma = pltpu.SemaphoreType.DMA
     return pl.pallas_call(
-        functools.partial(kernel, nrows, ncols),
+        body,
         out_shape=(
             jax.ShapeDtypeStruct((BLOCK, width), F32),
             jax.ShapeDtypeStruct((n_obs // ncols, width), F32),
@@ -423,13 +451,9 @@
         scratch_shapes=[
             pltpu.VMEM((nrows, 7, BLOCK), F32),
             pltpu.VMEM((ncols, 7, BLOCK), F32),
-            pltpu.VMEM((n_rows + n_obs, 48), BF),
-            pltpu.VMEM((n_rows, 48), BF),
         ]
-        + [pltpu.VMEM((48, n_cols), BF)] * 5
         + [pltpu.VMEM((n_cols // COLS, 4, BLOCK, width), BF)]
         + [pltpu.VMEM((ROWS, COLS), F32)] * 6
-        + [pltpu.VMEM((2 * n_cols // LANES, ROWS, LANES), BF)] * 2
         + [
             pltpu.VMEM((ROWS, width), F32),
             pltpu.VMEM((BLOCK, width), F32),

time: 81.7 us -> 90.2 us (1.10)
  the two profiles are of different devices: /device:TPU:26 before, /device:TPU:27 now
where the time goes in v3:
time: 90.2 us; the launch traced here: 90.1 us
  Pallas kernels  87.1 us (97%)
  local copies, waits for them, and re-layouts  2.33 us (3%)
    pallas_call x1, Pallas kernels, local(): pl.pallas_call(body, out_shape=(jax.ShapeDtypeStruct((BLOCK, width), F32)...  87.1 us
    unnamed x4, local copies, waits for them, and re-layouts  2.33 us

profile of v3, /device:TPU:27, one launch (start us, length us, event | category | flops | bytes accessed | tf_op | source)
XLA Modules:
  0.0 90.1 jit_solution(8309117424009772421)
XLA Ops:
  0.6 87.1 %burton_miller.1 = (f32[256,256]{1,0:T(8,128)}, f32[64,256]{1,0:T(8,128)}) custom-call(bf16[256,256]{1,0:T(8,128)(2,1)} %refs_0_.1, f32[7,256]{1,0:T(8,128)} %refs_1_.1, s32[8,256]{1,0:T(8,128)} %refs_2_.1, f32[16,256]{1,0:T(8,128)} %refs_3_.1, s32[1,128]{1,0:T(1,128)} %bitcast.2, s32[1,128]{1,0:T(1,128)} %bitcast.3, f32[2,8192]{1,0:T(2,128)} %refs_6_.1), custom_call_target="tpu_custom_call" | custom-call | tf_op jit(solution)/shard_map/burton_miller/pallas_call | solution.py:443
  87.7 0.0 copy-start
  87.7 1.7 %copy.11 = f32[256,256]{1,0:T(8,128)} copy(f32[256,256]{1,0:T(8,128)} %get-tuple-element.4) | data formatting | bytes 524288
  89.4 0.0 copy-done
  89.4 0.6 copy.12
Async XLA Ops:
  87.7 1.7 %copy-start = (f32[64,256]{1,0:T(8,128)S(1)}, f32[64,256]{1,0:T(8,128)}, u32[]{:S(2)}) copy-start(f32[64,256]{1,0:T(8,128)} %get-tuple-element.5) | copy-start | bytes 196612

commit v4 on v3

--- a/solution.py
+++ b/solution.py
@@ -184,16 +184,17 @@
 
 
 def kernel(
-    nrows, ncols, left_a, left_b, r0, r1, r2, r3, r4, t0, t1, t2,
+    nrows, ncols, left_a, left_b, r0, r1, r2, r3, r4, t0, t1, t2, t3,
     krylov, geometry, corr_index, corr_weight, blades, harmonic, angles,
     out, far_out,
-    cgeo, rgeo, x2, p0, p1, p2, p3, p4, p5, acc, base,
+    cgeo, rgeo, x2, p0, p1, p2, p3, p4, p5, acc, acc2, acc3, base,
     stage, far_stage, part_in, far_in,
     send_sem, cgeo_sem, rgeo_sem, x_sem, far_sem, part_sem,
 ):
     rights = (r0, r1, r2, r3, r4)
     planes = ((p0, p1, p2), (p3, p4, p5))
-    tiles = (t0, t1, t2)
+    tiles = (t0, t1, t2, t3)
+    accs = (acc, acc2, acc3)
     r = lax.axis_index("rows")
     c = lax.axis_index("cols")
     core = r % 2
@@ -249,6 +250,8 @@
     x = krylov[...]
     index = corr_index[...] - (r * ncols + c) * BLOCK
     base[...] = -0.5 * x.astype(F32) - correction(x, index, corr_weight[...])
+    own = jnp.concatenate([geometry[...], jnp.zeros((1, BLOCK), F32)], axis=0)
+    base[...] += incident(own, blades[...], harmonic[...])
 
     pl.semaphore_wait(barrier, nrows + ncols - 2)
     for k in range(1, nrows):
@@ -257,24 +260,21 @@
         send(geometry, cgeo.at[at], cgeo_sem.at[at], peer, c)
     for k in range(1, ncols):
         send(geometry, rgeo.at[c], rgeo_sem.at[c], r, (c + k) % ncols)
+
+    for k in range(1, nrows):
+        at = (chip + k) % nrows
+        arrived(cgeo.at[at], cgeo_sem.at[at])
+    for k in range(1, ncols):
+        at = (c + k) % ncols
+        arrived(rgeo.at[at], rgeo_sem.at[at])
     send(krylov, x2.at[(chips + chip) // 2, chip % 2], x_sem.at[chips + chip], sibling, c)
     for k in range(1, chips):
         peer = (chip + k) % chips * 2 + core
         send(krylov, x2.at[chip // 2, chip % 2], x_sem.at[chip], peer, c)
-
-    own = jnp.concatenate([geometry[...], jnp.zeros((1, BLOCK), F32)], axis=0)
-    base[...] += incident(own, blades[...], harmonic[...])
-
-    for k in range(1, nrows):
-        at = (chip + k) % nrows
-        arrived(cgeo.at[at], cgeo_sem.at[at])
     g = jnp.concatenate([cgeo[i] for i in range(nrows)], axis=1)
     g = jnp.concatenate([g, jnp.zeros((1, n_cols), F32)], axis=0)
     for ref, v in zip(rights, right_features(g)):
         ref[...] = v
-    for k in range(1, ncols):
-        at = (c + k) % ncols
-        arrived(rgeo.at[at], rgeo_sem.at[at])
     g = jnp.concatenate([rgeo[i] for i in range(ncols)], axis=1)
     g = jnp.concatenate([g, jnp.zeros((1, n_rows), F32)], axis=0)
     la, lb = left_features(g, 4.0 / panels)
@@ -307,75 +307,77 @@
         return dot(lhs, x2[step].reshape(2 * COLS, x2.shape[-1]))
 
     every = pl.ds(0, ROWS)
-    blocks = n_rows // ROWS
-    where = [(c // 2 + 1 + b) % blocks for b in range(blocks)]
+    pair = c // 2
+    far_z, near_z = (1 - pair // 2) * 2, pair // 2 * 2
+    where = [far_z + pair % 2, far_z + 1 - pair % 2, near_z + 1 - pair % 2, pair]
+    blocks = len(where)
     seq = [(n_rows, True)] + [(w * ROWS, False) for w in where]
-    lag = 2
+    multiplied = {3: (0, 1, 2), 4: (3,)}
 
     def prepare(step):
         for b in range(2):
             x2[step, 2 + b] = turned(x2[step, b])
 
-    def run(ph, first_h, last_h, extra=None):
-        gen, mul = ph < len(seq), ph >= lag
-
+    def run(ph, first_h, last_h):
         @pl.loop(first_h, last_h)
         def _(h):
             for par in range(2):
                 step = 2 * h + par
-                if gen:
-                    first, far = seq[ph]
-                    make_geometry(first, lax.rem(step + 1, steps), far, planes[1 - par])
-                    make_values(step, far, planes[par], tiles[ph % 3])
-                if extra is not None:
-                    extra(step)
-                if mul:
-                    acc[...] += product(step, tiles[(ph - lag) % 3], every)
-
-    def pass_on(step):
-        @pl.when(step > 0)
-        def _():
-            at = (chip + chips - step) % chips
+                first, far = seq[ph]
+                make_geometry(first, lax.rem(step + 1, steps), far, planes[1 - par])
+                make_values(step, far, planes[par], tiles[ph % 4])
+                for i, which in enumerate(multiplied.get(ph, ())):
+                    accs[i][...] += product(step, tiles[which % 4], every)
+
+    def pass_on():
+        for k in range(1, chips):
+            at = (chip + chips - k) % chips
             arrived(x2.at[at // 2, at % 2], x_sem.at[at])
-            forward(step, at).start()
-
-    def wait_and_prepare(step):
-        for b in range(2):
-            arrived(x2.at[step, b], x_sem.at[2 * step + b])
-        prepare(step)
+            forward(k, at).start()
+        for step in range(steps // 2):
+            prepare(step)
+
+    def take_passed():
+        for k in range(chips, nrows):
+            arrived(x2.at[k // 2, k % 2], x_sem.at[k])
+        for step in range(steps // 2, steps):
+            prepare(step)
 
     def send_parts(block):
         for b in range(2):
             owner = where[block] * 2 + b
             send(stage.at[owner], part_in.at[c], part_sem.at[c], r, owner)
 
-    for ph in range(len(seq) + 1):
-        if ph < len(seq):
-            first, far = seq[ph]
-            make_geometry(first, 0, far, planes[0])
-        if ph >= lag:
-            acc[...] = jnp.zeros_like(acc)
-        if ph == 3:
+    def keep_parts(block, total):
+        for b in range(2):
+            stage[where[block] * 2 + b] = total[pl.ds(b * BLOCK, BLOCK), :].astype(BF)
+
+    for ph in range(len(seq)):
+        first, far = seq[ph]
+        make_geometry(first, 0, far, planes[0])
+        for i in range(len(multiplied.get(ph, ()))):
+            accs[i][...] = jnp.zeros_like(accs[i])
+        if ph == 4:
             for k in range(1, ncols):
                 owner = (c + k) % ncols
                 rows = pl.ds(pl.multiple_of(owner * obs, obs), obs)
                 send(far_stage.at[rows, :], far_in.at[c], far_sem.at[c], r, owner)
-        if ph > 3:
-            send_parts(ph - 4)
-        if ph == 1:
-            run(ph, 0, steps // 2, pass_on)
-        elif ph == 2:
-            run(ph, 0, steps // 4, prepare)
-            run(ph, steps // 4, steps // 2, wait_and_prepare)
+            send_parts(0)
+            send_parts(1)
+        if ph == 3:
+            run(ph, 0, steps // 4)
+            take_passed()
+            run(ph, steps // 4, steps // 2)
+            far_stage[...] = accs[0][...]
+            keep_parts(0, accs[1])
+            keep_parts(1, accs[2])
         else:
             run(ph, 0, steps // 2)
         if ph == 2:
-            far_stage[...] = acc[...]
-        elif ph > 2:
-            for b in range(2):
-                stage[where[ph - 3] * 2 + b] = acc[pl.ds(b * BLOCK, BLOCK), :].astype(BF)
-
-    tile = tiles[(len(seq) - 1) % 3]
+            pass_on()
+    keep_parts(2, accs[0])
+
+    tile = tiles[(len(seq) - 1) % 4]
     same = lax.broadcasted_iota(jnp.int32, (BLOCK, LANES), 0)
     lane = lax.broadcasted_iota(jnp.int32, (BLOCK, LANES), 1)
     rows = pl.ds(pl.multiple_of(c % 2 * BLOCK, BLOCK), BLOCK)
@@ -385,7 +387,7 @@
             v = tile[at, rows, :].astype(F32)
             tile[at, rows, :] = jnp.where(same == lane + h * LANES, 0.0, v).astype(BF)
 
-    send_parts(blocks - 2)
+    send_parts(2)
     partner = c + 1 - 2 * (c % 2)
     mine = acc.at[pl.ds(0, BLOCK), :]
     theirs = acc.at[pl.ds(BLOCK, BLOCK), :]
@@ -432,7 +434,7 @@
     scoped = (
         [pltpu.VMEM((n_rows + n_obs, 48), BF), pltpu.VMEM((n_rows, 48), BF)]
         + [pltpu.VMEM((48, n_cols), BF)] * 5
-        + [pltpu.VMEM((2 * n_cols // LANES, ROWS, LANES), BF)] * 3
+        + [pltpu.VMEM((2 * n_cols // LANES, ROWS, LANES), BF)] * 4
     )
 
     def body(*refs):
@@ -456,6 +458,8 @@
         + [pltpu.VMEM((ROWS, COLS), F32)] * 6
         + [
             pltpu.VMEM((ROWS, width), F32),
+            pltpu.VMEM((ROWS, width), F32),
+            pltpu.VMEM((ROWS, width), F32),
             pltpu.VMEM((BLOCK, width), F32),
             pltpu.VMEM((ncols, BLOCK, width), BF),
             pltpu.VMEM((n_obs, width), F32),

time: 90.2 us -> 76.7 us (0.85)
  the two profiles are of different devices: /device:TPU:27 before, /device:TPU:1 now
where the time goes in v4:
time: 76.7 us; the launch traced here: 76.5 us
  Pallas kernels  73.5 us (96%)
  local copies, waits for them, and re-layouts  2.33 us (3%)
    pallas_call x1, Pallas kernels, local(): pl.pallas_call(body, out_shape=(jax.ShapeDtypeStruct((BLOCK, width), F32)...  73.5 us
    unnamed x4, local copies, waits for them, and re-layouts  2.33 us

profile of v4, /device:TPU:1, one launch (start us, length us, event | category | flops | bytes accessed | tf_op | source)
XLA Modules:
  0.0 76.5 jit_solution(9038479864021803888)
XLA Ops:
  0.6 73.5 %burton_miller.1 = (f32[256,256]{1,0:T(8,128)}, f32[64,256]{1,0:T(8,128)}) custom-call(bf16[256,256]{1,0:T(8,128)(2,1)} %refs_0_.1, f32[7,256]{1,0:T(8,128)} %refs_1_.1, s32[8,256]{1,0:T(8,128)} %refs_2_.1, f32[16,256]{1,0:T(8,128)} %refs_3_.1, s32[1,128]{1,0:T(1,128)} %bitcast.2, s32[1,128]{1,0:T(1,128)} %bitcast.3, f32[2,8192]{1,0:T(2,128)} %refs_6_.1), custom_call_target="tpu_custom_call" | custom-call | tf_op jit(solution)/shard_map/burton_miller/pallas_call | solution.py:445
  74.2 0.0 copy-start
  74.2 1.7 %copy.11 = f32[256,256]{1,0:T(8,128)} copy(f32[256,256]{1,0:T(8,128)} %get-tuple-element.4) | data formatting | bytes 524288
  75.9 0.0 copy-done
  75.9 0.6 copy.12
Async XLA Ops:
  74.2 1.7 %copy-start = (f32[64,256]{1,0:T(8,128)S(1)}, f32[64,256]{1,0:T(8,128)}, u32[]{:S(2)}) copy-start(f32[64,256]{1,0:T(8,128)} %get-tuple-element.5) | copy-start | bytes 196612

commit v5 on v4

--- a/solution.py
+++ b/solution.py
@@ -281,26 +281,30 @@
     left_a[pl.ds(0, n_rows), :] = la.T.astype(BF)
     left_b[...] = lb.T.astype(BF)
 
-    def make_geometry(first, step, far, into):
+    def make_geometry(panel, step, into):
+        first, far, count = panel
         cols = pl.ds(pl.multiple_of(step * COLS, COLS), COLS)
-        rows = pl.ds(pl.multiple_of(first, ROWS), ROWS)
+        rows = pl.ds(pl.multiple_of(first, BLOCK), count)
+        top = pl.ds(0, count)
         la = left_a[rows, :]
         if far:
-            into[0][...] = dot(la, rights[3][:, cols])
-            into[1][...] = dot(la, rights[4][:, cols])
+            into[0][top, :] = dot(la, rights[3][:, cols])
+            into[1][top, :] = dot(la, rights[4][:, cols])
         else:
-            into[0][...] = dot(la, rights[0][:, cols])
-            into[1][...] = dot(la, rights[1][:, cols])
-            into[2][...] = dot(left_b[rows, :], rights[2][:, cols])
-
-    def make_values(step, far, frm, tile):
+            into[0][top, :] = dot(la, rights[0][:, cols])
+            into[1][top, :] = dot(la, rights[1][:, cols])
+            into[2][top, :] = dot(left_b[rows, :], rights[2][:, cols])
+
+    def make_values(panel, step, frm, tile):
+        _, far, count = panel
+        top = pl.ds(0, count)
         if far:
-            re, im = far_values(frm[0][...], frm[1][...])
+            re, im = far_values(frm[0][top, :], frm[1][top, :])
         else:
-            re, im = operator_tile(frm[0][...], frm[1][...], frm[2][...])
+            re, im = operator_tile(frm[0][top, :], frm[1][top, :], frm[2][top, :])
         for h in range(half):
-            tile[step * 2 * half + h] = re[:, h * LANES : (h + 1) * LANES]
-            tile[step * 2 * half + half + h] = im[:, h * LANES : (h + 1) * LANES]
+            tile[step * 2 * half + h, top, :] = re[:, h * LANES : (h + 1) * LANES]
+            tile[step * 2 * half + half + h, top, :] = im[:, h * LANES : (h + 1) * LANES]
 
     def product(step, tile, rows):
         lhs = jnp.concatenate([tile[step * 2 * half + h, rows, :] for h in range(2 * half)], axis=1)
@@ -310,24 +314,28 @@
     pair = c // 2
     far_z, near_z = (1 - pair // 2) * 2, pair // 2 * 2
     where = [far_z + pair % 2, far_z + 1 - pair % 2, near_z + 1 - pair % 2, pair]
-    blocks = len(where)
-    seq = [(n_rows, True)] + [(w * ROWS, False) for w in where]
-    multiplied = {3: (0, 1, 2), 4: (3,)}
+    partner = c + 1 - 2 * (c % 2)
+    seq = [(n_rows, True, ROWS)] + [(w * ROWS, False, ROWS) for w in where[:-1]]
+    seq += [(partner * BLOCK, False, BLOCK), (c * BLOCK, False, BLOCK)]
 
     def prepare(step):
         for b in range(2):
             x2[step, 2 + b] = turned(x2[step, b])
 
-    def run(ph, first_h, last_h):
-        @pl.loop(first_h, last_h)
+    def two_steps(ph, h, products, between=None):
+        for par in range(2):
+            step = 2 * h + par
+            make_geometry(seq[ph], lax.rem(step + 1, steps), planes[1 - par])
+            if par == 0 and between is not None:
+                between()
+            make_values(seq[ph], step, planes[par], tiles[ph % 4])
+            for which, at, total, rows in products(step, par):
+                total[rows, :] += product(at, tiles[which % 4], rows)
+
+    def run(ph, products):
+        @pl.loop(0, steps // 2)
         def _(h):
-            for par in range(2):
-                step = 2 * h + par
-                first, far = seq[ph]
-                make_geometry(first, lax.rem(step + 1, steps), far, planes[1 - par])
-                make_values(step, far, planes[par], tiles[ph % 4])
-                for i, which in enumerate(multiplied.get(ph, ())):
-                    accs[i][...] += product(step, tiles[which % 4], every)
+            two_steps(ph, h, products)
 
     def pass_on():
         for k in range(1, chips):
@@ -352,59 +360,68 @@
         for b in range(2):
             stage[where[block] * 2 + b] = total[pl.ds(b * BLOCK, BLOCK), :].astype(BF)
 
+    def send_far():
+        for k in range(1, ncols):
+            owner = (c + k) % ncols
+            rows = pl.ds(pl.multiple_of(owner * obs, obs), obs)
+            send(far_stage.at[rows, :], far_in.at[c], far_sem.at[c], r, owner)
+
+    def catch_up(first):
+        listed = [(w, first + i, accs[w], every) for w in range(3) for i in range(steps // 2)]
+        each = len(listed) // (steps // 2)
+        return lambda h, par: listed[(2 * h + par) * each : (2 * h + par + 1) * each]
+
+    top = pl.ds(0, BLOCK)
     for ph in range(len(seq)):
-        first, far = seq[ph]
-        make_geometry(first, 0, far, planes[0])
-        for i in range(len(multiplied.get(ph, ()))):
-            accs[i][...] = jnp.zeros_like(accs[i])
-        if ph == 4:
-            for k in range(1, ncols):
-                owner = (c + k) % ncols
-                rows = pl.ds(pl.multiple_of(owner * obs, obs), obs)
-                send(far_stage.at[rows, :], far_in.at[c], far_sem.at[c], r, owner)
+        make_geometry(seq[ph], 0, planes[0])
+        if ph < 3:
+            run(ph, lambda step, par: ())
+            if ph == 2:
+                pass_on()
+        elif ph == 3:
+            for total in accs:
+                total[...] = jnp.zeros_like(total)
+            for part in range(2):
+                todo = catch_up(part * (steps // 2))
+                for h in range(steps // 4):
+                    last = part == 1 and h == 1
+                    if last:
+                        far_stage[...] = accs[0][...]
+                    two_steps(
+                        ph, part * (steps // 4) + h, lambda step, par, h=h, todo=todo: todo(h, par), send_far if last else None
+                    )
+                if part == 0:
+                    take_passed()
+            keep_parts(0, accs[1])
+            keep_parts(1, accs[2])
+        elif ph == 4:
+            accs[0][...] = jnp.zeros_like(accs[0])
             send_parts(0)
             send_parts(1)
-        if ph == 3:
-            run(ph, 0, steps // 4)
-            take_passed()
-            run(ph, steps // 4, steps // 2)
-            far_stage[...] = accs[0][...]
-            keep_parts(0, accs[1])
-            keep_parts(1, accs[2])
+            run(ph, lambda step, par: ((3, step, accs[0], every),))
+            keep_parts(2, accs[0])
         else:
-            run(ph, 0, steps // 2)
-        if ph == 2:
-            pass_on()
-    keep_parts(2, accs[0])
+            accs[1][top, :] = jnp.zeros((BLOCK, acc.shape[1]), F32)
+            send_parts(2)
+            run(ph, lambda step, par: ((4, step, accs[1], top),))
+            stage[partner] = accs[1][top, :].astype(BF)
 
     tile = tiles[(len(seq) - 1) % 4]
     same = lax.broadcasted_iota(jnp.int32, (BLOCK, LANES), 0)
     lane = lax.broadcasted_iota(jnp.int32, (BLOCK, LANES), 1)
-    rows = pl.ds(pl.multiple_of(c % 2 * BLOCK, BLOCK), BLOCK)
     for h in range(BLOCK // LANES):
         for part in range(2):
             at = chip // 2 * 2 * half + part * half + chip % 2 * (BLOCK // LANES) + h
-            v = tile[at, rows, :].astype(F32)
-            tile[at, rows, :] = jnp.where(same == lane + h * LANES, 0.0, v).astype(BF)
-
-    send_parts(2)
-    partner = c + 1 - 2 * (c % 2)
-    mine = acc.at[pl.ds(0, BLOCK), :]
-    theirs = acc.at[pl.ds(BLOCK, BLOCK), :]
-    other_rows = pl.ds(pl.multiple_of((1 - c % 2) * BLOCK, BLOCK), BLOCK)
-    theirs[...] = product(0, tile, other_rows)
+            v = tile[at, top, :].astype(F32)
+            tile[at, top, :] = jnp.where(same == lane + h * LANES, 0.0, v).astype(BF)
+
+    mine = acc.at[top, :]
+    mine[...] = product(0, tile, top)
+    send(stage.at[partner], part_in.at[c], part_sem.at[c], r, partner)
 
     @pl.loop(1, steps)
     def _(step):
-        theirs[...] += product(step, tile, other_rows)
-
-    stage[partner] = theirs[...].astype(BF)
-    mine[...] = product(0, tile, rows)
-    send(stage.at[partner], part_in.at[c], part_sem.at[c], r, partner)
-
-    @pl.loop(1, steps)
-    def _(step):
-        mine[...] += product(step, tile, rows)
+        mine[...] += product(step, tile, top)
 
     total = far_stage[pl.ds(pl.multiple_of(c * obs, obs), obs), :]
     for k in range(1, ncols):

time: 76.7 us -> 73.7 us (0.961)
  Pallas kernels: 73.5 us -> 70.5 us
    pallas_call x1, Pallas kernels: 73.5 us -> 70.5 us  [local(): pl.pallas_call(body, out_shape=(jax.ShapeDtypeStruct((BLOCK, width), F32)...]
where the time goes in v5:
time: 73.7 us; the launch traced here: 73.5 us
  Pallas kernels  70.5 us (96%)
  local copies, waits for them, and re-layouts  2.33 us (3%)
    pallas_call x1, Pallas kernels, local(): pl.pallas_call(body, out_shape=(jax.ShapeDtypeStruct((BLOCK, width), F32)...  70.5 us
    unnamed x4, local copies, waits for them, and re-layouts  2.33 us

profile of v5, /device:TPU:1, one launch (start us, length us, event | category | flops | bytes accessed | tf_op | source)
XLA Modules:
  0.0 73.5 jit_solution(17577648785411798547)
XLA Ops:
  0.6 70.5 %burton_miller.1 = (f32[256,256]{1,0:T(8,128)}, f32[64,256]{1,0:T(8,128)}) custom-call(bf16[256,256]{1,0:T(8,128)(2,1)} %refs_0_.1, f32[7,256]{1,0:T(8,128)} %refs_1_.1, s32[8,256]{1,0:T(8,128)} %refs_2_.1, f32[16,256]{1,0:T(8,128)} %refs_3_.1, s32[1,128]{1,0:T(1,128)} %bitcast.2, s32[1,128]{1,0:T(1,128)} %bitcast.3, f32[2,8192]{1,0:T(2,128)} %refs_6_.1), custom_call_target="tpu_custom_call" | custom-call | tf_op jit(solution)/shard_map/burton_miller/pallas_call | solution.py:462
  71.1 0.0 copy-start
  71.2 1.7 %copy.11 = f32[256,256]{1,0:T(8,128)} copy(f32[256,256]{1,0:T(8,128)} %get-tuple-element.4) | data formatting | bytes 524288
  72.9 0.0 copy-done
  72.9 0.6 copy.12
Async XLA Ops:
  71.1 1.7 %copy-start = (f32[64,256]{1,0:T(8,128)S(1)}, f32[64,256]{1,0:T(8,128)}, u32[]{:S(2)}) copy-start(f32[64,256]{1,0:T(8,128)} %get-tuple-element.5) | copy-start | bytes 196612

commit v6 on v5

--- a/solution.py
+++ b/solution.py
@@ -332,8 +332,8 @@
             for which, at, total, rows in products(step, par):
                 total[rows, :] += product(at, tiles[which % 4], rows)
 
-    def run(ph, products):
-        @pl.loop(0, steps // 2)
+    def run(ph, products, first_h=0, last_h=steps // 2):
+        @pl.loop(first_h, last_h)
         def _(h):
             two_steps(ph, h, products)
 
@@ -366,37 +366,37 @@
             rows = pl.ds(pl.multiple_of(owner * obs, obs), obs)
             send(far_stage.at[rows, :], far_in.at[c], far_sem.at[c], r, owner)
 
-    def catch_up(first):
-        listed = [(w, first + i, accs[w], every) for w in range(3) for i in range(steps // 2)]
-        each = len(listed) // (steps // 2)
-        return lambda h, par: listed[(2 * h + par) * each : (2 * h + par + 1) * each]
-
     top = pl.ds(0, BLOCK)
     for ph in range(len(seq)):
         make_geometry(seq[ph], 0, planes[0])
-        if ph < 3:
+        if ph < 2:
             run(ph, lambda step, par: ())
-            if ph == 2:
-                pass_on()
+        elif ph == 2:
+            run(ph, lambda step, par: (), 0, steps // 4)
+            pass_on()
+            accs[0][...] = jnp.zeros_like(accs[0])
+            run(ph, lambda step, par: ((0, step - steps // 2, accs[0], every),), steps // 4, steps // 2)
         elif ph == 3:
-            for total in accs:
+            take_passed()
+            for total in accs[1:]:
                 total[...] = jnp.zeros_like(total)
-            for part in range(2):
-                todo = catch_up(part * (steps // 2))
-                for h in range(steps // 4):
-                    last = part == 1 and h == 1
-                    if last:
-                        far_stage[...] = accs[0][...]
-                    two_steps(
-                        ph, part * (steps // 4) + h, lambda step, par, h=h, todo=todo: todo(h, par), send_far if last else None
-                    )
-                if part == 0:
-                    take_passed()
-            keep_parts(0, accs[1])
+            listed = [(0, at, accs[0], every) for at in range(steps // 2, steps)]
+            listed += [(w, at, accs[w], every) for w in (1, 2) for at in range(steps)]
+            each = len(listed) // (steps // 2)
+            more = (each + 1) // 2
+            for h in range(steps // 2):
+                todo = listed[h * each : (h + 1) * each]
+                between = None
+                if h == 1:
+                    far_stage[...] = accs[0][...]
+                    between = send_far
+                if h == 3:
+                    keep_parts(0, accs[1])
+                    between = functools.partial(send_parts, 0)
+                two_steps(ph, h, lambda step, par, todo=todo: todo[more:] if par else todo[:more], between)
             keep_parts(1, accs[2])
         elif ph == 4:
             accs[0][...] = jnp.zeros_like(accs[0])
-            send_parts(0)
             send_parts(1)
             run(ph, lambda step, par: ((3, step, accs[0], every),))
             keep_parts(2, accs[0])

time: 73.7 us -> 71.4 us (0.969)
  Pallas kernels: 70.5 us -> 68.2 us
    pallas_call x1, Pallas kernels: 70.5 us -> 68.2 us  [local(): pl.pallas_call(body, out_shape=(jax.ShapeDtypeStruct((BLOCK, width), F32)...]
where the time goes in v6:
time: 71.4 us; the launch traced here: 71.2 us
  Pallas kernels  68.2 us (96%)
  local copies, waits for them, and re-layouts  2.33 us (3%)
    pallas_call x1, Pallas kernels, local(): pl.pallas_call(body, out_shape=(jax.ShapeDtypeStruct((BLOCK, width), F32)...  68.2 us
    unnamed x4, local copies, waits for them, and re-layouts  2.33 us

profile of v6, /device:TPU:1, one launch (start us, length us, event | category | flops | bytes accessed | tf_op | source)
XLA Modules:
  0.0 71.2 jit_solution(14934298935639110333)
XLA Ops:
  0.6 68.2 %burton_miller.1 = (f32[256,256]{1,0:T(8,128)}, f32[64,256]{1,0:T(8,128)}) custom-call(bf16[256,256]{1,0:T(8,128)(2,1)} %refs_0_.1, f32[7,256]{1,0:T(8,128)} %refs_1_.1, s32[8,256]{1,0:T(8,128)} %refs_2_.1, f32[16,256]{1,0:T(8,128)} %refs_3_.1, s32[1,128]{1,0:T(1,128)} %bitcast.2, s32[1,128]{1,0:T(1,128)} %bitcast.3, f32[2,8192]{1,0:T(2,128)} %refs_6_.1), custom_call_target="tpu_custom_call" | custom-call | tf_op jit(solution)/shard_map/burton_miller/pallas_call | solution.py:462
  68.9 0.0 copy-start
  68.9 1.7 %copy.11 = f32[256,256]{1,0:T(8,128)} copy(f32[256,256]{1,0:T(8,128)} %get-tuple-element.4) | data formatting | bytes 524288
  70.6 0.0 copy-done
  70.6 0.6 copy.12
Async XLA Ops:
  68.9 1.7 %copy-start = (f32[64,256]{1,0:T(8,128)S(1)}, f32[64,256]{1,0:T(8,128)}, u32[]{:S(2)}) copy-start(f32[64,256]{1,0:T(8,128)} %get-tuple-element.5) | copy-start | bytes 196612
